TPU v7x, 32 devices: a whole 2x2x4 slice. The times are simulated.
32 devices in a mesh: tx: 2 (over x), rx: 4 (over z), freq: 4 (over y, core).
Axes of the slice: x: 2, y: 2, z: 4, core: 2. Of those that a mesh axis runs over, the one named last changes fastest.
Arguments:
- spectrum: float32 [2, 8, 2048, 2048], P(None, 'freq', 'tx', 'rx'), may hold values from -6 to 6
- measured: float32 [2, 8, 2048, 2048], P(None, 'freq', 'tx', 'rx'), may hold values from -12 to 12
- wavenumber: float32 [8], replicated, may hold values from 1.5 to 3
- send_weight: float32 [2048], P('tx'), may hold values from 0.25 to 2
- hear_weight: float32 [2048], P('rx'), may hold values from 0.25 to 2
- aperture: int32 [128, 128], P('tx', 'rx'), may hold values 0 or 1
Outputs:
- updated: float32 [2, 8, 2048, 2048], P(None, 'freq', 'tx', 'rx')
- residual: float32 [2, 8, 2048, 2048], P(None, 'freq', 'tx', 'rx')
Inputs may be any that keep to these rules, and one draw needn't show every extreme that they name: `aperture`: 1 marks a live tile of 16 x 16 antenna pairs, 0 a silent one.
All inputs are finite; a program needn't handle non-finite values. No bound on the sum of `aperture` on one device may be relied on, other than what follows from the above.
Results may differ from a plain program's by a relative error of at most 0.00016.
Values sent between devices are 32-bit elements; how exact they have to be, the bound alone decides.
A program may use at most 192 MiB of HBM per device.

v0:
```python
import math

import jax
import jax.numpy as jnp
from jax import lax
from jax.experimental import pallas as pl
from jax.sharding import PartitionSpec as P

depth_step = 2.0
step_size = 0.125
root_floor = 0.25
radix = 4


def roots(wavenumber, offset, length, total):
    indices = offset + jnp.arange(length, dtype=jnp.int32)
    signed = jnp.where(indices < total // 2, indices, indices - total)
    waves = 2.0 * jnp.pi / total * signed.astype(jnp.float32)
    squared = (wavenumber * wavenumber)[:, None] - (waves * waves)[None, :]
    return jnp.sqrt(jnp.maximum(squared, 0.0) + root_floor)


def unit_pair(outer, inner, period):
    product = (
        jnp.arange(outer, dtype=jnp.int32)[:, None] * jnp.arange(inner, dtype=jnp.int32)[None, :] % period
    )
    phases = 2.0 * math.pi / period * product.astype(jnp.float32)
    return jnp.cos(phases), jnp.sin(phases)


def dft_tables(total):
    width = total // radix
    base_cos, base_sin = unit_pair(width, width, width)
    turn_cos, turn_sin = unit_pair(radix, width, total)
    scale = 1.0 / math.sqrt(total)
    turn_cos = turn_cos[:, None, :] * scale
    turn_sin = turn_sin[:, None, :] * scale
    return (
        turn_cos * base_cos - turn_sin * base_sin,
        turn_cos * base_sin + turn_sin * base_cos,
    )


def dft(pieces, tables, form, sign):
    (ar, ai), (br, bi), (cr, ci), (dr, di) = [(x[0], x[1]) for x in pieces]
    er, ei, gr, gi = ar + cr, ai + ci, ar - cr, ai - ci
    hr, hi, kr, ki = br + dr, bi + di, sign * (br - dr), sign * (bi - di)
    mixed_real = jnp.stack([er + hr, gr - ki, er - hr, gr + ki])
    mixed_imag = jnp.stack([ei + hi, gi + kr, ei - hi, gi - kr])
    mixed = jnp.stack([mixed_real, mixed_imag], axis=1)
    cosine, sine = tables
    first = jnp.einsum(form, cosine, mixed, precision=lax.Precision.HIGH)
    second = jnp.einsum(form, sine, mixed, precision=lax.Precision.HIGH)
    return jnp.stack(
        [
            first[:, :, 0] - sign * second[:, :, 1],
            first[:, :, 1] + sign * second[:, :, 0],
        ]
    )


def unmix(done, blocks):
    total = done.shape[1] * done.shape[2]
    rows = total // math.prod(blocks)
    freqs, width = done.shape[3:]
    done = jnp.transpose(done, (2, 1, 0, 3, 4)).reshape((math.prod(blocks), rows, 2, freqs, width))
    return jnp.transpose(done, (0, 2, 3, 1, 4)).reshape(tuple(blocks) + (2, freqs, rows, width))


def quarters(chunks, axis):
    count = chunks.shape[0]
    if count >= radix and count % radix == 0:
        step = count // radix
        return [
            jnp.concatenate([chunks[q * step + k] for k in range(step)], axis=axis) for q in range(radix)
        ]
    whole = jnp.concatenate([chunks[k] for k in range(count)], axis=axis)
    return jnp.split(whole, radix, axis=axis)


def exchange(values, axes):
    return lax.all_to_all(values, axes, split_axis=0, concat_axis=0, tiled=True)


def pair_kernel(layers, sent, heard, out):
    depth, rows = layers.shape[1:3]
    for f in range(out.shape[1]):
        hr = heard[0, f : f + 1, :]
        hi = heard[1, f : f + 1, :]
        for start in range(0, rows, 8):
            block = slice(start, start + 8)
            sr = sent[0, block, f : f + 1]
            si = sent[1, block, f : f + 1]
            zr = sr * hr - si * hi
            zi = -(sr * hi + si * hr)
            ar = layers[0, depth - 1, block, :]
            ai = layers[1, depth - 1, block, :]
            for j in range(depth - 1, -1, -1):
                ar, ai = ar * zr - ai * zi, ar * zi + ai * zr
                if j:
                    ar = ar + layers[0, j - 1, block, :]
                    ai = ai + layers[1, j - 1, block, :]
            out[0, f, block, :] = ar
            out[1, f, block, :] = ai


def gradient_kernel(pieces, sent, heard, out):
    freqs, rows = pieces.shape[1:3]
    depth = out.shape[1]
    for start in range(0, rows, 8):
        block = slice(start, start + 8)
        sums = [None] * depth
        for f in range(freqs):
            hr = heard[0, f : f + 1, :]
            hi = heard[1, f : f + 1, :]
            sr = sent[0, block, f : f + 1]
            si = sent[1, block, f : f + 1]
            zr = sr * hr - si * hi
            zi = sr * hi + si * hr
            tr = step_size * pieces[0, f, block, :]
            ti = step_size * pieces[1, f, block, :]
            for j in range(depth):
                tr, ti = tr * zr - ti * zi, tr * zi + ti * zr
                if f:
                    sums[j] = (sums[j][0] + tr, sums[j][1] + ti)
                else:
                    sums[j] = (tr, ti)
        for j in range(depth):
            out[0, j, block, :] = sums[j][0]
            out[1, j, block, :] = sums[j][1]


def pointwise(kernel, values, sent, heard, planes):
    _, count, rows, width = values.shape
    freqs = heard.shape[1]
    height = min(rows, 32)
    lanes = min(width, 128)
    return pl.pallas_call(
        kernel,
        grid=(rows // height, width // lanes),
        in_specs=[
            pl.BlockSpec((2, count, height, lanes), lambda i, k: (0, 0, i, k)),
            pl.BlockSpec((2, height, freqs), lambda i, k: (0, i, 0)),
            pl.BlockSpec((2, freqs, lanes), lambda i, k: (0, 0, k)),
        ],
        out_specs=pl.BlockSpec((2, planes, height, lanes), lambda i, k: (0, 0, i, k)),
        out_shape=jax.ShapeDtypeStruct((2, planes, rows, width), jnp.float32),
    )(values, sent, heard)


def per_device(spectrum, measured, wavenumber, send_weight, hear_weight, aperture):
    _, depth_local, rows_sent, rows_heard = spectrum.shape
    freq_local = measured.shape[1]
    freq_total = wavenumber.shape[0]
    senders = lax.axis_size("tx")
    hearers = lax.axis_size("rx")
    layers = lax.axis_size("freq")
    depth = depth_local * layers
    total_sent = rows_sent * senders
    total_heard = rows_heard * hearers
    slab = rows_sent // layers
    strip = rows_heard // senders
    band = rows_sent // hearers

    first_row = lax.axis_index("tx") * rows_sent + lax.axis_index("freq") * slab
    sent_phase = depth_step * roots(wavenumber, first_row, slab, total_sent).T
    heard_phase = depth_step * roots(wavenumber, lax.axis_index("rx") * rows_heard, rows_heard, total_heard)
    sent = jnp.stack([jnp.cos(sent_phase), jnp.sin(sent_phase)])
    heard = jnp.stack([jnp.cos(heard_phase), jnp.sin(heard_phase)])
    tables_sent = dft_tables(total_sent)
    tables_heard = tables_sent if total_heard == total_sent else dft_tables(total_heard)
    near = "qsm,qcfmw->qscfw"
    far = "qsm,qcfwm->qscfw"

    split = spectrum.reshape(2, depth_local, layers, slab, rows_heard)
    split = exchange(jnp.transpose(split, (2, 0, 1, 3, 4)), "freq")
    stacked = jnp.transpose(split, (1, 0, 2, 3, 4)).reshape(2, depth, slab, rows_heard)
    pair = pointwise(pair_kernel, stacked, sent, heard, freq_total)

    pair = pair.reshape(2, layers, freq_local, slab, senders, strip)
    pair = jnp.transpose(pair, (4, 1, 0, 2, 3, 5)).reshape(senders * layers, 2, freq_local, slab, strip)
    pair = exchange(pair, ("tx", "freq"))
    done = dft(quarters(pair, 2), tables_sent, near, 1.0)
    done = exchange(unmix(done, (senders * hearers,)), ("tx", "rx"))
    done = done.reshape((senders, hearers) + done.shape[1:])
    done = jnp.swapaxes(done, 0, 1).reshape((senders * hearers,) + done.shape[2:])
    done = dft(quarters(done, 3), tables_heard, far, 1.0)
    done = exchange(unmix(done, (hearers,)), "rx")
    field = jnp.transpose(done, (1, 2, 0, 4, 3)).reshape(2, freq_local, rows_sent, rows_heard)

    tiles_sent, tiles_heard = aperture.shape
    gate = aperture.astype(jnp.float32)
    weights = (
        send_weight.reshape(tiles_sent, -1)[:, :, None, None]
        * gate[:, None, :, None]
        * hear_weight.reshape(tiles_heard, -1)[None, None, :, :]
    ).reshape(rows_sent, rows_heard)
    residual = weights[None, None] * (measured - field)

    back = residual.reshape(2, freq_local, hearers, band, rows_heard)
    back = exchange(jnp.transpose(back, (2, 0, 1, 3, 4)), "rx")
    done = dft(quarters(back, 3), tables_heard, far, -1.0)
    done = unmix(done, (hearers, senders))
    done = jnp.swapaxes(done, 0, 1).reshape((senders * hearers,) + done.shape[2:])
    done = exchange(done, ("tx", "rx"))
    done = dft(quarters(done, 3), tables_sent, far, -1.0)
    done = exchange(unmix(done, (senders * layers,)), ("tx", "freq"))
    done = done.reshape(senders, layers, 2, freq_local, slab, strip)
    pieces = jnp.transpose(done, (2, 1, 3, 4, 0, 5)).reshape(2, freq_total, slab, rows_heard)

    gradient = pointwise(gradient_kernel, pieces, sent, heard, depth)
    gradient = gradient.reshape(2, layers, depth_local, slab, rows_heard)
    gradient = exchange(jnp.transpose(gradient, (1, 0, 2, 3, 4)), "freq")
    gradient = jnp.transpose(gradient, (1, 2, 0, 3, 4)).reshape(spectrum.shape)
    return (spectrum + gradient, residual)


def solution(mesh):
    placed = (
        P(None, "freq", "tx", "rx"),
        P(None, "freq", "tx", "rx"),
        P(),
        P("tx"),
        P("rx"),
        P("tx", "rx"),
    )
    return jax.shard_map(
        per_device,
        mesh=mesh,
        in_specs=placed,
        out_specs=(P(None, "freq", "tx", "rx"), P(None, "freq", "tx", "rx")),
        check_vma=False,
    )
```

profile of v0, /device:TPU:19, one launch (start us, length us, event | category | flops | bytes accessed | tf_op | source)
XLA Modules:
  0.0 1439.9 jit_solution(16936419594886305284)
XLA Ops:
  0.6 8.1 copy.126
  8.8 6.4 all-to-all-start
  17.0 90.4 %all-to-all-done = f32[4,2,2,256,512]{4,3,2,1,0:T(8,128)} async-done(((f32[4,2,2,256,512]{4,3,2,1,0:T(8,128)}), f32[4,2,2,256,512]{4,3,2,1,0:T(8,128)}, u32[]{:S(2)}, u32[]{:S(2)}) %all-to-all-start) | async-done | bytes 8388640 | tf_op jit(solution)/shard_map/all_to_all | solution.py:82
  107.4 8.1 copy.127
  115.5 24.7 %shard_map.77 = f32[2,8,256,512]{3,2,1,0:T(8,128)} custom-call(f32[2,8,256,512]{3,2,1,0:T(8,128)} %bitcast.225, f32[2,256,8]{2,1,0:T(8,128)} %copy.128.sent, f32[2,8,512]{2,1,0:T(8,128)} %pad_maximum_fusion.20.heard), custom_call_target="tpu_custom_call" | custom-call | tf_op jit(solution)/shard_map/pallas_call | solution.py:138
  140.2 10.5 reshape.804
  150.7 7.9 copy.129
  158.7 6.0 all-to-all-start.1
  164.7 4.1 fusion.85
  168.8 87.2 %all-to-all-done.1 = f32[8,2,2,256,256]{4,3,2,1,0:T(8,128)} async-done(((f32[8,2,2,256,256]{4,3,2,1,0:T(8,128)}), f32[8,2,2,256,256]{4,3,2,1,0:T(8,128)}, u32[]{:S(2)}, u32[]{:S(2)}) %all-to-all-start.1) | async-done | bytes 8388640 | tf_op jit(solution)/shard_map/all_to_all | solution.py:82
  256.0 3.9 slice_bitcast_fusion.24
  263.2 7.2 fusion.9
  270.4 7.4 fusion.10
  282.9 4.0 maximum_bitcast_fusion
  286.9 9.2 copy.133
  296.1 186.0 %all_to_all.40 = f32[8,2,2,256,256]{4,2,1,3,0:T(2,128)S(1)} all-to-all(f32[8,2,2,256,256]{4,2,1,3,0:T(2,128)S(1)} %bitcast.227), channel_id=1, replica_groups=mesh['tx'=2,'rx'=4,'freq'=4] {'tx','rx'}, dimensions={0} | all-to-all | bytes 16777216 | tf_op jit(solution)/shard_map/all_to_all | solution.py:82
  489.0 7.3 fusion.7
  496.3 7.1 fusion.8
  506.5 2.7 maximum_bitcast_fusion.1
  509.3 11.1 copy.139
  520.4 7.8 all-to-all-start.3
  528.6 8.5 mul.580
  537.1 14.9 %mul.581 = f32[1024,512]{1,0:T(8,128)} reshape(f32[64,16,32,16]{3,2,1,0:T(8,128)} %mul.580) | data formatting | bytes 4194304 | tf_op jit(solution)/shard_map/mul | solution.py:194
  552.0 3.2 broadcast_multiply_fusion
  555.2 152.6 %all-to-all-done.3 = f32[4,2,2,512,256]{4,2,1,3,0:T(2,128)} async-done(((f32[4,2,2,512,256]{4,2,1,3,0:T(2,128)}), f32[4,2,2,512,256]{4,2,1,3,0:T(2,128)}, u32[]{:S(2)}, u32[]{:S(2)}) %all-to-all-start.3) | async-done | bytes 8388640 | tf_op jit(solution)/shard_map/all_to_all | solution.py:82
  707.8 13.1 copy.140
  720.9 12.1 fusion
  733.0 4.4 copy.184
  737.4 185.9 %all_to_all.41 = f32[4,2,2,256,512]{4,3,2,1,0:T(8,128)S(1)} all-to-all(f32[4,2,2,256,512]{4,3,2,1,0:T(8,128)S(1)} %bitcast.235), channel_id=1, replica_groups=mesh['tx'=2,'rx'=4,'freq'=4] {'rx'}, dimensions={0} | all-to-all | bytes 16777216 | tf_op jit(solution)/shard_map/all_to_all | solution.py:82
  926.4 7.1 fusion.31
  933.5 7.3 fusion.1
  941.3 2.6 fusion.17
  943.9 2.7 maximum_bitcast_fusion.2
  946.6 9.2 copy.147
  958.2 186.8 %all_to_all.42 = f32[8,2,2,256,256]{4,3,2,1,0:T(8,128)S(1)} all-to-all(f32[8,2,2,256,256]{4,3,2,1,0:T(8,128)S(1)} %bitcast.231), channel_id=1, replica_groups=mesh['tx'=2,'rx'=4,'freq'=4] {'tx','rx'}, dimensions={0} | all-to-all | bytes 16777216 | tf_op jit(solution)/shard_map/all_to_all | solution.py:82
  1149.5 7.1 fusion.3
  1156.6 7.3 fusion.5
  1163.9 3.9 fusion.14
  1167.8 4.0 maximum_bitcast_fusion.3
  1171.8 9.2 copy.155
  1181.1 97.4 %all_to_all.43 = f32[8,2,2,256,256]{4,2,1,3,0:T(2,128)S(1)} all-to-all(f32[8,2,2,256,256]{4,2,1,3,0:T(2,128)S(1)} %bitcast.232), channel_id=1, replica_groups=mesh['tx'=2,'rx'=4,'freq'=4] {'tx','freq'}, dimensions={0} | all-to-all | bytes 16777216 | tf_op jit(solution)/shard_map/all_to_all | solution.py:82
  1280.0 8.0 copy.157
  1288.0 11.6 reshape.817.pieces
  1299.5 24.7 %shard_map.78 = f32[2,8,256,512]{3,2,1,0:T(8,128)} custom-call(f32[2,8,256,512]{3,2,1,0:T(8,128)} %reshape.817.pieces, f32[2,256,8]{2,1,0:T(8,128)} %copy.128.sent, f32[2,8,512]{2,1,0:T(8,128)} %pad_maximum_fusion.20.heard), custom_call_target="tpu_custom_call" | custom-call | tf_op jit(solution)/shard_map/pallas_call | solution.py:138
  1324.3 4.4 copy.183
  1328.7 95.4 %all_to_all.44 = f32[4,2,2,256,512]{4,3,2,1,0:T(8,128)S(1)} all-to-all(f32[4,2,2,256,512]{4,3,2,1,0:T(8,128)S(1)} %bitcast.234), channel_id=1, replica_groups=mesh['tx'=2,'rx'=4,'freq'=4] {'freq'}, dimensions={0} | all-to-all | bytes 16777216 | tf_op jit(solution)/shard_map/all_to_all | solution.py:82
  1424.1 4.3 copy.160
  1428.4 11.3 bitcast_add_fusion
  (54 shorter events, 32.2 us)
Async XLA Ops:
  8.8 6.4 copy-start.3
  8.8 98.6 %all-to-all-start = ((f32[4,2,2,256,512]{4,3,2,1,0:T(8,128)}), f32[4,2,2,256,512]{4,3,2,1,0:T(8,128)}, u32[]{:S(2)}, u32[]{:S(2)}) async-start(f32[4,2,2,256,512]{4,3,2,1,0:T(8,128)} %copy.126), calls=%async_computation | async-start | bytes 16777216 | tf_op jit(solution)/shard_map/all_to_all | solution.py:82
  158.7 97.3 %all-to-all-start.1 = ((f32[8,2,2,256,256]{4,3,2,1,0:T(8,128)}), f32[8,2,2,256,256]{4,3,2,1,0:T(8,128)}, u32[]{:S(2)}, u32[]{:S(2)}) async-start(f32[8,2,2,256,256]{4,3,2,1,0:T(8,128)} %bitcast.222), calls=%async_computation.1 | async-start | bytes 16777216 | tf_op jit(solution)/shard_map/all_to_all | solution.py:82
  520.4 7.8 copy-start
  520.4 7.9 copy-start.1
  520.4 187.4 %all-to-all-start.3 = ((f32[4,2,2,512,256]{4,2,1,3,0:T(2,128)}), f32[4,2,2,512,256]{4,2,1,3,0:T(2,128)}, u32[]{:S(2)}, u32[]{:S(2)}) async-start(f32[4,2,2,512,256]{4,2,1,3,0:T(2,128)} %bitcast.221), calls=%async_computation.3 | async-start | bytes 16777216 | tf_op jit(solution)/shard_map/all_to_all | solution.py:82
  537.1 14.9 %copy-start.2 = (f32[512]{0:T(512)S(1)}, f32[512]{0:T(512)}, u32[]{:S(2)}) copy-start(f32[512]{0:T(512)} %param.10) | copy-start | bytes 6148
where the time goes:
time: 1460 us; the launch traced here: 1440 us
  blocking collectives  752 us (52%)
  waiting for transfers between devices  330 us (23%)
  local copies, waits for them, and re-layouts  156 us (11%)
  other arithmetic  73.9 us (5%)
  matrix products  57.7 us (4%)
  Pallas kernels  49.4 us (3%)
  starting transfers between devices  20.2 us (1%)
    all_to_all x5, blocking collectives, exchange(): return lax.all_to_all(values, axes, split_axis=0, concat_axis=0, tiled=True)  752 us
    all_to_all x3, waiting for transfers between devices, exchange(): return lax.all_to_all(values, axes, split_axis=0, concat_axis=0, tiled=True)  330 us
    pallas_call x2, Pallas kernels, pointwise(): pl.pallas_call(kernel, grid=(rows // height, width // lanes), in_specs=[p...  49.4 us
    transpose x4, local copies, waits for them, and re-layouts, unmix(): jnp.transpose(done, (2, 1, 0, 3, 4))  38.8 us
  transfers between devices with their start and end apart: 3, of which 3 were waited for; matrix products, arithmetic and copies ran while one was open for 2% of the time, Pallas kernels for 0%

commit v1 on v0

--- a/solution.py
+++ b/solution.py
@@ -1,15 +1,19 @@
+import functools
 import math
 
 import jax
 import jax.numpy as jnp
 from jax import lax
 from jax.experimental import pallas as pl
+from jax.experimental.pallas import tpu as pltpu
 from jax.sharding import PartitionSpec as P
+
 
 depth_step = 2.0
 step_size = 0.125
 root_floor = 0.25
 radix = 4
+limit = 60 << 20
 
 
 def roots(wavenumber, offset, length, total):
@@ -215,6 +219,540 @@
     return (spectrum + gradient, residual)
 
 
+lanes = 128
+chunks = 2
+
+
+def split(values):
+    high = values.astype(jnp.bfloat16)
+    return high, (values - high.astype(jnp.float32)).astype(jnp.bfloat16)
+
+
+def split_table(values):
+    high = lax.reduce_precision(values, 8, 7)
+    return high.astype(jnp.bfloat16), (values - high).astype(jnp.bfloat16)
+
+
+def stacked_tables(total):
+    width = total // radix
+    base = unit_pair(width, width, width)
+    turn = unit_pair(radix, width, total)
+    scale = 1.0 / math.sqrt(total)
+    forms = []
+    for where in ((slice(None), None, slice(None)), (slice(None), slice(None), None)):
+        turn_cos, turn_sin = turn[0][where] * scale, turn[1][where] * scale
+        cosine = turn_cos * base[0] - turn_sin * base[1]
+        sine = turn_cos * base[1] + turn_sin * base[0]
+        forms.append(jnp.stack(split_table(cosine) + split_table(sine), axis=1))
+    return forms
+
+
+def turned(table, s, high, low, left):
+    def times(values, kind):
+        pair = (table[s, kind], values) if left else (values, table[s, kind])
+        return jnp.dot(*pair, preferred_element_type=jnp.float32)
+
+    first = times(high, 0) + (times(high, 1) + times(low, 0))
+    second = times(high, 2) + (times(high, 3) + times(low, 2))
+    return first, second
+
+
+def mix(parts, sign):
+    (ar, ai), (br, bi), (cr, ci), (dr, di) = parts
+    er, ei, gr, gi = ar + cr, ai + ci, ar - cr, ai - ci
+    hr, hi, kr, ki = br + dr, bi + di, sign * (br - dr), sign * (bi - di)
+    return (er + hr, ei + hi), (gr - ki, gi + kr), (er - hr, ei - hi), (gr + ki, gi - kr)
+
+
+def aligned(index, size):
+    return pl.ds(pl.multiple_of(index * size, size), size)
+
+
+def phase_of(sent, heard, f, rows, columns):
+    hr, hi = heard[0, f : f + 1, columns], heard[1, f : f + 1, columns]
+    sr, si = sent[0, rows, f : f + 1], sent[1, rows, f : f + 1]
+    return sr * hr - si * hi, sr * hi + si * hr
+
+
+def pair_rows_kernel(local, step, layers, sent, heard, table, *rest):
+    out, high, low = rest[-3:]
+    hearers, groups, _, per, rows, width = layers.shape
+    senders, part = out.shape[0], width // hearers
+    turns = radix // senders
+    spans = width // lanes
+    block = groups * rows
+    for g in range(groups):
+        f = g * local + step
+
+        def body(t, carry):
+            row, span = t // spans, t % spans
+            down, across = aligned(row, 16), aligned(span, lanes)
+            parts = []
+            for h in range(hearers):
+                zr, zi = phase_of(sent, heard, f, down, aligned(h * spans + span, lanes))
+                ar = layers[h, groups - 1, 0, per - 1, down, across]
+                ai = layers[h, groups - 1, 1, per - 1, down, across]
+                for j in range(groups * per - 1, -1, -1):
+                    ar, ai = ar * zr + ai * zi, ai * zr - ar * zi
+                    if j:
+                        q, d = divmod(j - 1, per)
+                        ar = ar + layers[h, q, 0, d, down, across]
+                        ai = ai + layers[h, q, 1, d, down, across]
+                parts.append((ar, ai))
+            for s, values in enumerate(mix(parts, 1.0)):
+                for c in range(2):
+                    place = aligned((c * block + g * rows) // 16 + row, 16)
+                    high[s, place, across], low[s, place, across] = split(values[c])
+            return carry
+
+        lax.fori_loop(0, rows // 16 * spans, body, 0)
+    for s in range(radix):
+        first, second = turned(table, s, high[s], low[s], False)
+        real = first[:block] - second[block:]
+        imag = first[block:] + second[:block]
+        columns = slice(s % turns * part, (s % turns + 1) * part)
+        for g in range(groups):
+            for p in range(hearers):
+                piece = (slice(g * rows, (g + 1) * rows), slice(p * part, (p + 1) * part))
+                out[s // turns, p, g, 0, :, columns] = real[piece]
+                out[s // turns, p, g, 1, :, columns] = imag[piece]
+
+
+def pair_rows(layers, sent, heard, table, local, step, senders, before, count, chunk):
+    hearers, groups, _, per, rows, width = layers.shape
+    height = min(rows, 32)
+    strip = width // senders
+    freqs = groups * local
+    first = chunk * (rows // height)
+    return pl.pallas_call(
+        functools.partial(pair_rows_kernel, local, step),
+        grid=(rows // height,),
+        in_specs=[
+            pl.BlockSpec((hearers, groups, 2, per, height, width), lambda i: (0, 0, 0, 0, i, 0)),
+            pl.BlockSpec((2, height, freqs), lambda i: (0, i, 0)),
+            pl.BlockSpec((2, freqs, hearers * width), lambda i: (0, 0, 0)),
+            pl.BlockSpec(table.shape, lambda i: (0, 0, 0, 0), pipeline_mode=pl.Buffered(1)),
+        ]
+        + [pl.BlockSpec(memory_space=pl.ANY)] * (before is not None),
+        out_specs=pl.BlockSpec(
+            (senders, hearers, groups, 2, height, strip), lambda i: (0, 0, 0, 0, i + first, 0)
+        ),
+        out_shape=jax.ShapeDtypeStruct((senders, hearers, groups, 2, rows * count, strip), jnp.float32),
+        scratch_shapes=[pltpu.VMEM((radix, 2 * groups * height, width), jnp.bfloat16)] * 2,
+        input_output_aliases={} if before is None else {4: 0},
+        compiler_params=pltpu.CompilerParams(vmem_limit_bytes=limit),
+        cost_estimate=pl.CostEstimate(flops=6 * 10**9, bytes_accessed=24 << 20, transcendentals=0),
+    )(layers, sent, heard, table, *([] if before is None else [before]))
+
+
+def gradient_rows_kernel(local, step, pieces, sent, heard, table, *rest):
+    before = rest[0] if len(rest) == 5 else None
+    out, high, low, done = rest[-4:]
+    senders, hearers, groups, _, rows, _ = pieces.shape
+    width, per = out.shape[5], out.shape[3]
+    part = width // hearers
+    turns = radix // senders
+    spans = width // lanes
+    block = groups * rows
+    for s in range(radix):
+        columns = slice(s % turns * part, (s % turns + 1) * part)
+        for g in range(groups):
+            for c in range(2):
+                down = slice(c * block + g * rows, c * block + (g + 1) * rows)
+                for p in range(hearers):
+                    across = slice(p * part, (p + 1) * part)
+                    values = pieces[s // turns, p, g, c, :, columns]
+                    high[s, down, across], low[s, down, across] = split(values)
+    for s in range(radix):
+        first, second = turned(table, s, high[s], low[s], False)
+        done[s, 0] = first[:block] + second[block:]
+        done[s, 1] = first[block:] - second[:block]
+
+    def body(t, carry):
+        row, span = t // spans, t % spans
+        across = aligned(span, lanes)
+        for g in range(groups):
+            down = aligned(g * rows // 8 + row, 8)
+            parts = [(done[s, 0, down, across], done[s, 1, down, across]) for s in range(radix)]
+            for h, (real, imag) in enumerate(mix(parts, -1.0)):
+                done[h, 0, down, across] = step_size * real
+                done[h, 1, down, across] = step_size * imag
+        here = aligned(row, 8)
+        for h in range(hearers):
+            sums = [None] * (groups * per)
+            for g in range(groups):
+                zr, zi = phase_of(sent, heard, g * local + step, here, aligned(h * spans + span, lanes))
+                down = aligned(g * rows // 8 + row, 8)
+                tr, ti = done[h, 0, down, across], done[h, 1, down, across]
+                for j in range(groups * per):
+                    tr, ti = tr * zr - ti * zi, tr * zi + ti * zr
+                    sums[j] = (sums[j][0] + tr, sums[j][1] + ti) if g else (tr, ti)
+            for j in range(groups * per):
+                q, d = divmod(j, per)
+                for c in range(2):
+                    value = sums[j][c]
+                    if before is not None:
+                        value = value + before[h, q, c, d, here, across]
+                    out[h, q, c, d, here, across] = value
+        return carry
+
+    lax.fori_loop(0, rows // 8 * spans, body, 0)
+
+
+def gradient_rows(pieces, sent, heard, table, before, local, step, per, chunk):
+    senders, hearers, groups, _, _, strip = pieces.shape
+    rows = sent.shape[1]
+    width = strip * senders
+    height = min(rows, 32)
+    first = chunk * (rows // height)
+    freqs = groups * local
+    cube = pl.BlockSpec((hearers, groups, 2, per, height, width), lambda i: (0, 0, 0, 0, i, 0))
+    return pl.pallas_call(
+        functools.partial(gradient_rows_kernel, local, step),
+        grid=(rows // height,),
+        in_specs=[
+            pl.BlockSpec((senders, hearers, groups, 2, height, strip), lambda i: (0, 0, 0, 0, i + first, 0)),
+            pl.BlockSpec((2, height, freqs), lambda i: (0, i, 0)),
+            pl.BlockSpec((2, freqs, hearers * width), lambda i: (0, 0, 0)),
+            pl.BlockSpec(table.shape, lambda i: (0, 0, 0, 0), pipeline_mode=pl.Buffered(1)),
+        ]
+        + [cube] * (before is not None),
+        out_specs=cube,
+        out_shape=jax.ShapeDtypeStruct((hearers, groups, 2, per, rows, width), jnp.float32),
+        scratch_shapes=[pltpu.VMEM((radix, 2 * groups * height, width), jnp.bfloat16)] * 2
+        + [pltpu.VMEM((radix, 2, groups * height, width), jnp.float32)],
+        compiler_params=pltpu.CompilerParams(vmem_limit_bytes=limit),
+        cost_estimate=pl.CostEstimate(flops=6 * 10**9, bytes_accessed=24 << 20, transcendentals=0),
+    )(pieces, sent, heard, table, *([] if before is None else [before]))
+
+
+def columns_kernel(count, parts_out, senders, place, *refs):
+    ins, refs = refs[:count], refs[count:]
+    seen, refs = refs[:senders], refs[senders:]
+    weights, refs = refs[:senders], refs[senders:]
+    ahead, behind, refs = refs[0], refs[1], refs[2:]
+    outs, refs = refs[:parts_out], refs[parts_out:]
+    left, refs = refs[:senders], refs[senders:]
+    high, low, field = refs
+    devices, _, rows, _ = ins[0].shape
+    groups = devices // radix
+    width = high.shape[1]
+    rest = width // senders
+    me = place[0]
+
+    def gather(d, carry):
+        for n in range(count):
+            parts = [(ins[n][q * groups + d, 0], ins[n][q * groups + d, 1]) for q in range(radix)]
+            down = aligned(d * count + n, rows)
+            for s, values in enumerate(mix(parts, 1.0)):
+                for c in range(2):
+                    across = slice(c * lanes, (c + 1) * lanes)
+                    high[s, down, across], low[s, down, across] = split(values[c])
+        return carry
+
+    lax.fori_loop(0, groups, gather, 0)
+    for s in range(radix):
+        first, second = turned(ahead, s, high[s], low[s], True)
+        field[s, :, :lanes] = first[:, :lanes] - second[:, lanes:]
+        field[s, :, lanes:] = first[:, lanes:] + second[:, :lanes]
+        for shift in range(senders):
+            down = aligned(lax.rem(me + senders - shift, senders), rest)
+            weight = weights[shift][0, s]
+            for c in range(2):
+                across = slice(c * lanes, (c + 1) * lanes)
+                values = weight * (seen[shift][c, s] - field[s, down, across])
+                left[shift][c, s] = values
+                high[s, down, across], low[s, down, across] = split(values)
+    for s in range(radix):
+        first, second = turned(behind, s, high[s], low[s], True)
+        field[s, :, :lanes] = first[:, :lanes] + second[:, lanes:]
+        field[s, :, lanes:] = first[:, lanes:] - second[:, :lanes]
+
+    def scatter(d, carry):
+        for n in range(parts_out):
+            down = aligned(d * parts_out + n, rows * count // parts_out)
+            parts = [(field[s, down, :lanes], field[s, down, lanes:]) for s in range(radix)]
+            for q, values in enumerate(mix(parts, -1.0)):
+                for c in range(2):
+                    outs[n][q * groups + d, c] = values[c]
+        return carry
+
+    lax.fori_loop(0, groups, scatter, 0)
+
+
+def columns(pieces, seen, ahead, behind, step, place, parts_out):
+    count, senders = len(pieces), len(seen)
+    devices, _, rows, strip = pieces[0].shape
+    planes, _, rest, _ = seen[0].shape
+    width = rest * senders
+    moved = pl.BlockSpec((devices, 2, rows, lanes), lambda i, place: (0, 0, 0, i))
+    short = rows * count // parts_out
+    sent_on = pl.BlockSpec((devices, 2, short, lanes), lambda i, place: (0, 0, 0, i))
+    table = pl.BlockSpec(ahead.shape, lambda i, place: (0, 0, 0, 0), pipeline_mode=pl.Buffered(1))
+    outs = pl.pallas_call(
+        functools.partial(columns_kernel, count, parts_out, senders),
+        grid_spec=pltpu.PrefetchScalarGridSpec(
+            num_scalar_prefetch=1,
+            grid=(strip // lanes,),
+            in_specs=[moved] * count
+            + [pl.BlockSpec((2, radix, rest, lanes), lambda i, place: (step, 0, 0, i))] * senders
+            + [pl.BlockSpec((1, radix, rest, lanes), lambda i, place: (planes - 1, 0, 0, i))] * senders
+            + [table, table],
+            out_specs=[sent_on] * parts_out
+            + [pl.BlockSpec((2, radix, rest, lanes), lambda i, place: (0, 0, 0, i))] * senders,
+            scratch_shapes=[pltpu.VMEM((radix, width, 2 * lanes), jnp.bfloat16)] * 2
+            + [pltpu.VMEM((radix, width, 2 * lanes), jnp.float32)],
+        ),
+        out_shape=[jax.ShapeDtypeStruct((devices, 2, short, strip), jnp.float32)] * parts_out
+        + [jax.ShapeDtypeStruct((2, radix, rest, strip), jnp.float32)] * senders,
+        compiler_params=pltpu.CompilerParams(vmem_limit_bytes=limit),
+        cost_estimate=pl.CostEstimate(flops=12 * 10**9, bytes_accessed=36 << 20, transcendentals=0),
+    )(place, *pieces, *seen, *[x for x in seen], ahead, behind)
+    return outs[:parts_out], outs[parts_out:]
+
+
+def moved_exactly(values, table):
+    high = values.astype(jnp.bfloat16)
+    rest = values - high.astype(jnp.float32)
+    middle = rest.astype(jnp.bfloat16)
+    low = (rest - middle.astype(jnp.float32)).astype(jnp.bfloat16)
+    first, second, third = [jnp.dot(x, table, preferred_element_type=jnp.float32) for x in (high, middle, low)]
+    return (first + second) + third
+
+
+def spread_kernel(senders, place, measured, send, hear, gate, table, *outs):
+    outs, held = outs[:-1], outs[-1]
+    _, local, rows, width = measured.shape
+    strip = width // senders
+    part = width // radix
+    turns = radix // senders
+    tall = rows // radix
+    me = place[0]
+    spans = [slice(k * lanes, (k + 1) * lanes) for k in range(width // lanes)]
+    for f in range(local):
+        for c in range(2):
+            for k, across in enumerate(spans):
+                held[k] = measured[c, f, :, across]
+            for s in range(radix):
+                picked = pl.ds(s, tall, stride=radix)
+                values = jnp.concatenate([held[k, picked, :] for k in range(len(spans))], axis=1)
+                for shift in range(senders):
+                    target = lax.rem(me + shift, senders)
+                    outs[shift][2 * f + c, s] = moved_exactly(values, table[:, aligned(target, strip)])
+    for shift in range(senders):
+        target = lax.rem(me + shift, senders)
+        for s in range(radix):
+            for n in range(turns):
+                across = slice(n * part, (n + 1) * part)
+                outer = send[s] * hear[target * turns + n]
+                outs[shift][2 * local, s, :, across] = outer * gate[...]
+
+
+def spread(measured, send, hear, gate, table, place, senders):
+    _, local, rows, width = measured.shape
+    height = min(rows, 256)
+    strip = width // senders
+    rest, tall = rows // radix, height // radix
+    part = width // radix
+    return pl.pallas_call(
+        functools.partial(spread_kernel, senders),
+        grid_spec=pltpu.PrefetchScalarGridSpec(
+            num_scalar_prefetch=1,
+            grid=(rows // height,),
+            in_specs=[
+                pl.BlockSpec((2, local, height, width), lambda i, place: (0, 0, i, 0)),
+                pl.BlockSpec((radix, tall, 1), lambda i, place: (0, i, 0)),
+                pl.BlockSpec((radix, 1, part), lambda i, place: (0, 0, 0)),
+                pl.BlockSpec((tall, part), lambda i, place: (i, 0)),
+                pl.BlockSpec((width, width), lambda i, place: (0, 0)),
+            ],
+            out_specs=[pl.BlockSpec((2 * local + 1, radix, tall, strip), lambda i, place: (0, 0, i, 0))] * senders,
+            scratch_shapes=[pltpu.VMEM((width // lanes, height, lanes), jnp.float32)],
+        ),
+        out_shape=[jax.ShapeDtypeStruct((2 * local + 1, radix, rest, strip), jnp.float32)] * senders,
+        compiler_params=pltpu.CompilerParams(vmem_limit_bytes=limit),
+        cost_estimate=pl.CostEstimate(flops=6 * 10**9, bytes_accessed=18 << 20, transcendentals=0),
+    )(place, measured, send, hear, gate, table)
+
+
+def join_kernel(local, senders, place, *refs):
+    ins, table, out, held = refs[: local * senders], refs[-3], refs[-2], refs[-1]
+    tall, strip = ins[0].shape[2:]
+    spans = [slice(k * lanes, (k + 1) * lanes) for k in range(strip * senders // lanes)]
+    me = place[0]
+    for f in range(local):
+        for c in range(2):
+            for s in range(radix):
+                total = None
+                for shift in range(senders):
+                    source = lax.rem(me + shift, senders)
+                    moved = moved_exactly(ins[f * senders + shift][c, s], table[aligned(source, strip), :])
+                    total = moved if total is None else total + moved
+                for k, across in enumerate(spans):
+                    held[k, pl.ds(s, tall, stride=radix), :] = total[:, across]
+            for k, across in enumerate(spans):
+                out[c, f, :, across] = held[k]
+
+
+def join(pieces, table, place):
+    local, senders = len(pieces), len(pieces[0])
+    _, _, rest, strip = pieces[0][0].shape
+    rows, width = rest * radix, strip * senders
+    height = min(rows, 256)
+    return pl.pallas_call(
+        functools.partial(join_kernel, local, senders),
+        grid_spec=pltpu.PrefetchScalarGridSpec(
+            num_scalar_prefetch=1,
+            grid=(rows // height,),
+            in_specs=[pl.BlockSpec((2, radix, height // radix, strip), lambda i, place: (0, 0, i, 0))]
+            * (local * senders)
+            + [pl.BlockSpec((width, width), lambda i, place: (0, 0))],
+            out_specs=pl.BlockSpec((2, local, height, width), lambda i, place: (0, 0, i, 0)),
+            scratch_shapes=[pltpu.VMEM((width // lanes, height, lanes), jnp.float32)],
+        ),
+        out_shape=jax.ShapeDtypeStruct((2, local, rows, width), jnp.float32),
+        compiler_params=pltpu.CompilerParams(vmem_limit_bytes=limit),
+        cost_estimate=pl.CostEstimate(flops=6 * 10**9, bytes_accessed=16 << 20, transcendentals=0),
+    )(place, *[x for group in pieces for x in group], table)
+
+
+def add_kernel(spectrum, moved, *rest):
+    for k in range(moved.shape[0]):
+        rest[-1][:, :, k, 0] = spectrum[:, :, k, 0] + moved[k]
+
+
+def add(spectrum, moved, before, chunk):
+    groups, _, per, rows, width = moved.shape
+    count = spectrum.shape[2] // (groups * rows)
+    spectrum = spectrum.reshape(2, per, groups, count, rows, width)
+    some = math.gcd(groups, 2)
+    block = pl.BlockSpec((2, per, some, 1, rows, width), lambda i: (0, 0, i, chunk, 0, 0))
+    return pl.pallas_call(
+        add_kernel,
+        grid=(groups // some,),
+        in_specs=[block, pl.BlockSpec((some, 2, per, rows, width), lambda i: (i, 0, 0, 0, 0))]
+        + [pl.BlockSpec(memory_space=pl.ANY)] * (before is not None),
+        out_specs=block,
+        out_shape=jax.ShapeDtypeStruct(spectrum.shape, jnp.float32),
+        input_output_aliases={} if before is None else {2: 0},
+        cost_estimate=pl.CostEstimate(flops=2 * 10**6, bytes_accessed=12 << 20, transcendentals=0),
+    )(spectrum, moved, *([] if before is None else [before]))
+
+
+def passed(values, axis, way):
+    count = lax.axis_size(axis)
+    return [values[0]] + [
+        lax.ppermute(values[shift], axis, [(k, (k + way * shift) % count) for k in range(count)])
+        for shift in range(1, count)
+    ]
+
+
+def per_device_tiled(spectrum, measured, wavenumber, send_weight, hear_weight, aperture):
+    _, per, rows_sent, rows_heard = spectrum.shape
+    local = measured.shape[1]
+    senders = lax.axis_size("tx")
+    hearers = lax.axis_size("rx")
+    layers = lax.axis_size("freq")
+    total_sent = rows_sent * senders
+    total_heard = rows_heard * hearers
+    groups = hearers * layers
+    slab = rows_sent // groups
+    rows = slab // chunks
+    place = lax.axis_index("tx").reshape(1).astype(jnp.int32)
+
+    first_row = lax.axis_index("tx") * rows_sent + (lax.axis_index("rx") * layers + lax.axis_index("freq")) * slab
+    sent_phase = depth_step * roots(wavenumber, first_row, slab, total_sent).T
+    heard_phase = depth_step * roots(wavenumber, 0, total_heard, total_heard)
+    sent = jnp.stack([jnp.cos(sent_phase), jnp.sin(sent_phase)])
+    heard = jnp.stack([jnp.cos(heard_phase), jnp.sin(heard_phase)])
+    sents = [sent[:, n * rows : (n + 1) * rows] for n in range(chunks)]
+    ahead_sent, behind_sent = stacked_tables(total_sent)
+    ahead_heard, behind_heard = (
+        (ahead_sent, behind_sent) if total_heard == total_sent else stacked_tables(total_heard)
+    )
+
+    order = jnp.arange(rows_heard, dtype=jnp.int32)
+    order = order % (rows_heard // radix) * radix + order // (rows_heard // radix)
+    picks = (jnp.arange(rows_heard, dtype=jnp.int32)[:, None] == order[None, :]).astype(jnp.bfloat16)
+    tile_sent = rows_sent // aperture.shape[0] // radix
+    tile_heard = rows_heard // aperture.shape[1] // radix
+    gate = jnp.repeat(jnp.repeat(aperture, tile_sent, axis=0), tile_heard, axis=1).astype(jnp.float32)
+    send = send_weight.reshape(-1, radix).T[:, :, None]
+    hear = hear_weight.reshape(-1, radix).T[:, None, :]
+
+    everyone = ("tx", "rx", "freq")
+    cube = (hearers, layers, 2, per, rows, rows_heard)
+
+    def flat(x):
+        return x.reshape((senders * hearers * layers,) + x.shape[3:])
+
+    def boxed(x):
+        return x.reshape((senders, hearers, layers) + x.shape[1:])
+
+    blocks = spectrum.reshape(2, per, groups, chunks, rows, rows_heard)
+    arrived = []
+    for n in range(chunks):
+        block = jnp.transpose(blocks[:, :, :, n], (2, 0, 1, 3, 4))
+        arrived.append(exchange(block, ("rx", "freq")).reshape(cube))
+    seen = spread(measured, send, hear, gate, picks, place, senders)
+    seen = passed(seen, "tx", 1)
+
+    def pair_of(f, n, before, count):
+        where = n if count > 1 else 0
+        return pair_rows(
+            arrived[n], sents[n], heard, behind_heard, local, f, senders, before, count, where
+        )
+
+    pairs = []
+    for f in range(local):
+        if f == 0:
+            made = [pair_of(f, n, None, 1) for n in range(chunks)]
+        else:
+            whole = None
+            for n in range(chunks):
+                whole = pair_of(f, n, whole, chunks)
+            made = [whole]
+        moved = []
+        for x in made:
+            moved.append(exchange(flat(x), everyone))
+        pairs.append(moved)
+    residuals = []
+    gradient = [None] * chunks
+    for f in range(local):
+        count = chunks if f == local - 1 else 1
+        backs, left = columns(pairs[f], seen, ahead_sent, behind_sent, f, place, count)
+        residuals.append(passed(left, "tx", -1))
+        moved = []
+        for n in range(count):
+            moved.append(boxed(exchange(backs[n], everyone)))
+        for n in range(chunks):
+            pieces, where = (moved[n], 0) if count > 1 else (moved[0], n)
+            gradient[n] = gradient_rows(
+                pieces, sents[n], heard, ahead_heard, gradient[n], local, f, per, where
+            )
+    updated = None
+    moved = []
+    for n in range(chunks):
+        flat_gradient = gradient[n].reshape(groups, 2, per, rows, rows_heard)
+        moved.append(exchange(flat_gradient, ("rx", "freq")))
+    for n in range(chunks):
+        updated = add(spectrum, moved[n], updated, n)
+    residual = join(residuals, picks.T, place)
+    return (updated.reshape(spectrum.shape), residual)
+
+
+def fits(mesh, sent, heard):
+    senders, hearers, layers = [mesh.shape[axis] for axis in ("tx", "rx", "freq")]
+    rows = sent // senders // (hearers * layers)
+    return (
+        hearers == radix
+        and radix % senders == 0
+        and rows % (32 * chunks) == 0
+        and heard // hearers // radix % lanes == 0
+        and sent // senders % 256 == 0
+    )
+
+
 def solution(mesh):
     placed = (
         P(None, "freq", "tx", "rx"),
@@ -224,8 +762,14 @@
         P("rx"),
         P("tx", "rx"),
     )
+
+    def body(*args):
+        sent, heard = args[3].shape[0] * mesh.shape["tx"], args[4].shape[0] * mesh.shape["rx"]
+        local = args[1].shape[1]
+        return (per_device_tiled if fits(mesh, sent, heard) and local == 2 else per_device)(*args)
+
     return jax.shard_map(
-        per_device,
+        body,
         mesh=mesh,
         in_specs=placed,
         out_specs=(P(None, "freq", "tx", "rx"), P(None, "freq", "tx", "rx")),

time: 1460 us -> 926 us (0.63)
  blocking collectives: 752 us -> 98.5 us
  Pallas kernels: 49.4 us -> 224 us
  waiting for transfers between devices: 330 us -> 489 us
  local copies, waits for them, and re-layouts: 156 us -> 23.2 us
  matrix products: 57.7 us -> 0 us
  other arithmetic: 73.9 us -> 22.3 us
  starting transfers between devices: 20.2 us -> 55.7 us
    all_to_all x5 -> x1, blocking collectives: 752 us -> 98.5 us  [exchange(): return lax.all_to_all(values, axes, split_axis=0, concat_axis=0, tiled=True)]
    pallas_call x2 -> x14, Pallas kernels: 49.4 us -> 224 us  [the longest x4 58.1 us: pair_rows(): pl.pallas_call(functools.partial(pair_rows_kernel, local, step), grid=(ro...]
    ppermute x0 -> x3, waiting for transfers between devices: none -> 168 us  [passed(): lax.ppermute(values[shift], axis, [(k, (k + way * shift) % count) for k i...]
    transpose x12 -> x3, local copies, waits for them, and re-layouts: 87.3 us -> 14.5 us  [per_device_tiled(): block = jnp.transpose(blocks[:, :, :, n], (2, 0, 1, 3, 4))]
    dot_general x8 -> x0, matrix products: 57.7 us -> none  [the longest x4 28.9 us: dft(): second = jnp.einsum(form, sine, mixed, precision=lax.Precision.HIGH)]
    all_to_all x3 -> x9, starting transfers between devices: 20.2 us -> 53.9 us  [exchange(): return lax.all_to_all(values, axes, split_axis=0, concat_axis=0, tiled=True)]
    reshape x4 -> x3, local copies, waits for them, and re-layouts: 30.9 us -> 0.9 us  [the longest x2 0.77 us: per_device_tiled(): hear = hear_weight.reshape(-1, radix).T[:, None, :]]
    mul x3 -> x0, local copies, waits for them, and re-layouts: 23.5 us -> none  [per_device(): send_weight.reshape(tiles_sent, -1)[:, :, None, None]]
  transfers between devices with their start and end apart: 3 -> 12, of which waited for: 3 -> 10; matrix products, arithmetic and copies ran while one was open for 2% -> 4% of each run, Pallas kernels for 0% -> 24%
where the time goes in v1:
time: 926 us; the launch traced here: 914 us
  waiting for transfers between devices  489 us (53%)
  Pallas kernels  224 us (24%)
  blocking collectives  98.5 us (11%)
  starting transfers between devices  55.7 us (6%)
  local copies, waits for them, and re-layouts  23.2 us (3%)
  other arithmetic  22.3 us (2%)
    all_to_all x9, waiting for transfers between devices, exchange(): return lax.all_to_all(values, axes, split_axis=0, concat_axis=0, tiled=True)  321 us
    ppermute x3, waiting for transfers between devices, passed(): lax.ppermute(values[shift], axis, [(k, (k + way * shift) % count) for k i...  168 us
    all_to_all x1, blocking collectives, exchange(): return lax.all_to_all(values, axes, split_axis=0, concat_axis=0, tiled=True)  98.5 us
    pallas_call x4, Pallas kernels, pair_rows(): pl.pallas_call(functools.partial(pair_rows_kernel, local, step), grid=(ro...  58.1 us
    pallas_call x4, Pallas kernels, gradient_rows(): pl.pallas_call(functools.partial(gradient_rows_kernel, local, step), grid...  55.8 us
    all_to_all x9, starting transfers between devices, exchange(): return lax.all_to_all(values, axes, split_axis=0, concat_axis=0, tiled=True)  53.9 us
    pallas_call x2, Pallas kernels, columns(): pl.pallas_call(functools.partial(columns_kernel, count, parts_out, sender...  51.4 us
    pallas_call x1, Pallas kernels, join(): pl.pallas_call(functools.partial(join_kernel, local, senders), grid_spec=...  21.8 us
  transfers between devices with their start and end apart: 12, of which 10 were waited for; matrix products, arithmetic and copies ran while one was open for 4% of the time, Pallas kernels for 24%

profile of v1, /device:TPU:19, one launch (start us, length us, event | category | flops | bytes accessed | tf_op | source)
XLA Modules:
  0.0 913.5 jit_solution(8107340492073747849)
XLA Ops:
  0.6 6.9 slice_bitcast_fusion
  7.6 2.5 copy.33
  10.1 6.5 all-to-all-start
  16.6 5.0 copy.35
  21.6 87.1 %all-to-all-done = f32[16,2,2,32,512]{4,3,2,1,0:T(8,128)} async-done(((f32[16,2,2,32,512]{4,3,2,1,0:T(8,128)}), f32[16,2,2,32,512]{4,3,2,1,0:T(8,128)}, u32[]{:S(2)}, u32[]{:S(2)}) %all-to-all-start) | async-done | bytes 4194336 | tf_op jit(solution)/shard_map/all_to_all | solution.py:86
  108.7 5.2 all-to-all-start.1
  114.1 0.7 copy.45.sent
  114.9 4.1 fusion.12
  120.0 5.3 reduce-precision_convert_fusion.1
  125.3 3.8 pad_maximum_fusion.table.refs_6_.refs_7_
  129.1 14.5 %shard_map.82 = f32[2,4,4,2,32,256]{5,4,3,2,1,0:T(8,128)} custom-call(f32[4,4,2,2,32,512]{5,4,3,2,1,0:T(8,128)} %bitcast.4.layers, f32[2,32,8]{2,1,0:T(8,128)} %copy.45.sent, f32[2,8,2048]{2,1,0:T(8,128)} %pad_maximum_fusion.2.heard, bf16[4,4,512,512]{3,2,1,0:T(8,128)(2,1)} %pad_maximum_fusion.table.refs_6_.refs_7_), custom_call_target="tpu_custom_call" | custom-call | flops 6000000000 | bytes 25165824 | tf_op jit(solution)/shard_map/pallas_call | solution.py:327
  143.6 62.3 %all-to-all-done.1 = f32[16,2,2,32,512]{4,3,2,1,0:T(8,128)} async-done(((f32[16,2,2,32,512]{4,3,2,1,0:T(8,128)}), f32[16,2,2,32,512]{4,3,2,1,0:T(8,128)}, u32[]{:S(2)}, u32[]{:S(2)}) %all-to-all-start.1) | async-done | bytes 4194336 | tf_op jit(solution)/shard_map/all_to_all | solution.py:86
  205.9 5.3 all-to-all-start.5
  211.9 14.5 %shard_map.77.rest_0_ = f32[2,4,4,2,64,256]{5,4,3,2,1,0:T(8,128)} custom-call(f32[4,4,2,2,32,512]{5,4,3,2,1,0:T(8,128)} %bitcast.7.layers, f32[2,32,8]{2,1,0:T(8,128)} %copy.46.sent, f32[2,8,2048]{2,1,0:T(8,128)} %pad_maximum_fusion.2.heard, bf16[4,4,512,512]{3,2,1,0:T(8,128)(2,1)} %pad_maximum_fusion.table.refs_6_.refs_7_), custom_call_target="tpu_custom_call" | custom-call | flops 6000000000 | bytes 25165824 | tf_op jit(solution)/shard_map/pallas_call | solution.py:327
  226.4 14.5 %shard_map.78 = f32[2,4,4,2,64,256]{5,4,3,2,1,0:T(8,128)} custom-call(f32[4,4,2,2,32,512]{5,4,3,2,1,0:T(8,128)} %bitcast.4.layers, f32[2,32,8]{2,1,0:T(8,128)} %copy.45.sent, f32[2,8,2048]{2,1,0:T(8,128)} %pad_maximum_fusion.2.heard, bf16[4,4,512,512]{3,2,1,0:T(8,128)(2,1)} %pad_maximum_fusion.table.refs_6_.refs_7_, ...), custom_call_target="tpu_custom_call", output_to_operand_aliasing={{}: (4, {})} | custom-call | flops 6000000000 | bytes 25165824 | tf_op jit(solution)/shard_map/pallas_call | solution.py:327
  241.0 17.3 %all-to-all-done.5.refs_1_ = f32[32,2,32,256]{3,2,1,0:T(8,128)} async-done(((f32[32,2,32,256]{3,2,1,0:T(8,128)}), f32[32,2,32,256]{3,2,1,0:T(8,128)}, u32[]{:S(2)}, u32[]{:S(2)}) %all-to-all-start.5) | async-done | bytes 2097184 | tf_op jit(solution)/shard_map/all_to_all | solution.py:86
  258.3 6.5 all-to-all-start.2
  265.8 0.8 copy.42.gate
  266.7 2.7 copy.41.send
  269.4 1.2 fusion.11
  270.6 21.4 %shard_map.79 = (f32[5,4,256,256]{3,2,1,0:T(8,128)}, f32[5,4,256,256]{3,2,1,0:T(8,128)}) custom-call(s32[1]{0:T(128)} %bitcast.1.place, f32[2,2,1024,512]{3,2,1,0:T(8,128)} %measured.1, f32[4,256,1]{2,1,0:T(8,128)} %copy.41.send, f32[4,1,128]{2,1,0:T(1,128)} %bitcast.45, f32[256,128]{1,0:T(8,128)} %copy.42.gate, bf16[512,512]{1,0:T(8,128)(2,1)} %get-tuple-element.35.table), custom_call_target="tpu_custom_call" | custom-call | flops 6000000000 | bytes 18874368 | tf_op jit(solution)/shard_map/pallas_call | solution.py:557
  292.3 14.5 %shard_map.81 = f32[2,4,4,2,32,256]{5,4,3,2,1,0:T(8,128)} custom-call(f32[4,4,2,2,32,512]{5,4,3,2,1,0:T(8,128)} %bitcast.7.layers, f32[2,32,8]{2,1,0:T(8,128)} %copy.46.sent, f32[2,8,2048]{2,1,0:T(8,128)} %pad_maximum_fusion.2.heard, bf16[4,4,512,512]{3,2,1,0:T(8,128)(2,1)} %pad_maximum_fusion.table.refs_6_.refs_7_), custom_call_target="tpu_custom_call" | custom-call | flops 6000000000 | bytes 25165824 | tf_op jit(solution)/shard_map/pallas_call | solution.py:327
  306.8 50.2 %all-to-all-done.2.refs_0_ = f32[32,2,64,256]{3,2,1,0:T(8,128)} async-done(((f32[32,2,64,256]{3,2,1,0:T(8,128)}), f32[32,2,64,256]{3,2,1,0:T(8,128)}, u32[]{:S(2)}, u32[]{:S(2)}) %all-to-all-start.2) | async-done | bytes 4194336 | tf_op jit(solution)/shard_map/all_to_all | solution.py:86
  357.0 6.6 all-to-all-start.4
  363.6 6.6 pad_maximum_fusion.1.refs_5_.refs_6_.table
  370.3 77.0 %collective-permute-done.refs_2_.refs_4_.refs_3_.refs_5_ = f32[5,4,256,256]{3,2,1,0:T(8,128)} collective-permute-done((f32[5,4,256,256]{3,2,1,0:T(8,128)}, f32[5,4,256,256]{3,2,1,0:T(8,128)}, u32[]{:S(2)}, u32[]{:S(2)}) %collective-permute-start) | collective-permute-done | bytes 5242912 | tf_op jit(solution)/shard_map/ppermute | solution.py:645
  447.2 25.6 %shard_map.80 = (f32[32,2,32,256]{3,2,1,0:T(8,128)}, f32[32,2,32,256]{3,2,1,0:T(8,128)}, f32[2,4,256,256]{3,2,1,0:T(8,128)}, f32[2,4,256,256]{3,2,1,0:T(8,128)}) custom-call(s32[1]{0:T(128)} %bitcast.1.place, f32[32,2,64,256]{3,2,1,0:T(8,128)} %all-to-all-done.2.refs_0_, f32[5,4,256,256]{3,2,1,0:T(8,128)} %get-tuple-element.11.refs_1_.refs_3_.refs_2_.refs_4_, ...), custom_call_target="tpu_custom_call" | custom-call | flops 12000000000 | bytes 37748736 | tf_op jit(solution)/shard_map/pallas_call | solution.py:492
  472.9 5.6 all-to-all-start.8
  478.5 25.8 %shard_map.83 = (f32[32,2,64,256]{3,2,1,0:T(8,128)}, f32[2,4,256,256]{3,2,1,0:T(8,128)}, f32[2,4,256,256]{3,2,1,0:T(8,128)}) custom-call(s32[1]{0:T(128)} %bitcast.1.place, f32[32,2,32,256]{3,2,1,0:T(8,128)} %all-to-all-done.4.refs_0_, f32[32,2,32,256]{3,2,1,0:T(8,128)} %all-to-all-done.5.refs_1_, ...), custom_call_target="tpu_custom_call" | custom-call | flops 12000000000 | bytes 37748736 | tf_op jit(solution)/shard_map/pallas_call | solution.py:492
  504.3 21.4 %all-to-all-done.8 = f32[32,2,32,256]{3,2,1,0:T(8,128)S(1)} async-done(((f32[32,2,32,256]{3,2,1,0:T(8,128)}), f32[32,2,32,256]{3,2,1,0:T(8,128)S(1)}, u32[]{:S(2)}, u32[]{:S(2)}) %all-to-all-start.8) | async-done | bytes 2097184 | tf_op jit(solution)/shard_map/all_to_all | solution.py:86
  525.7 98.5 %all_to_all.50 = f32[32,2,64,256]{3,2,1,0:T(8,128)} all-to-all(f32[32,2,64,256]{3,2,1,0:T(8,128)} %get-tuple-element.14), channel_id=1, replica_groups=mesh['tx'=2,'rx'=4,'freq'=4] {'tx','rx','freq'}, dimensions={0} | all-to-all | bytes 8388608 | tf_op jit(solution)/shard_map/all_to_all | solution.py:86
  624.3 5.9 all-to-all-start.3
  630.1 13.2 %shard_map.86.rest_0_ = f32[4,4,2,2,32,512]{5,4,3,2,1,0:T(8,128)} custom-call(f32[2,4,4,2,64,256]{5,4,3,2,1,0:T(8,128)} %bitcast.35, f32[2,32,8]{2,1,0:T(8,128)} %copy.46.sent, f32[2,8,2048]{2,1,0:T(8,128)} %pad_maximum_fusion.2.heard, bf16[4,4,512,512]{3,2,1,0:T(8,128)(2,1)} %pad_maximum_fusion.1.refs_5_.refs_6_.table), custom_call_target="tpu_custom_call" | custom-call | flops 6000000000 | bytes 25165824 | tf_op jit(solution)/shard_map/pallas_call | solution.py:410
  643.3 14.8 %shard_map.87 = f32[4,4,2,2,32,512]{5,4,3,2,1,0:T(8,128)} custom-call(f32[2,4,4,2,32,256]{5,4,3,2,1,0:T(8,128)} %bitcast.40, f32[2,32,8]{2,1,0:T(8,128)} %copy.46.sent, f32[2,8,2048]{2,1,0:T(8,128)} %pad_maximum_fusion.2.heard, bf16[4,4,512,512]{3,2,1,0:T(8,128)(2,1)} %pad_maximum_fusion.1.refs_5_.refs_6_.table, f32[4,4,2,2,32,512]{5,4,3,2,1,0:T(8,128)} %shard_map.86.rest_0_), custom_call_target="tpu_custom_call" | custom-call | flops 6000000000 | bytes 25165824 | tf_op jit(solution)/shard_map/pallas_call | solution.py:410
  658.0 19.1 %all-to-all-done.3 = f32[32,2,32,256]{3,2,1,0:T(8,128)S(1)} async-done(((f32[32,2,32,256]{3,2,1,0:T(8,128)}), f32[32,2,32,256]{3,2,1,0:T(8,128)S(1)}, u32[]{:S(2)}, u32[]{:S(2)}) %all-to-all-start.3) | async-done | bytes 2097184 | tf_op jit(solution)/shard_map/all_to_all | solution.py:86
  677.1 1.3 copy-done.1
  678.4 6.8 all-to-all-start.9
  685.2 13.1 %shard_map.84.rest_0_ = f32[4,4,2,2,32,512]{5,4,3,2,1,0:T(8,128)} custom-call(f32[2,4,4,2,64,256]{5,4,3,2,1,0:T(8,128)} %bitcast.36, f32[2,32,8]{2,1,0:T(8,128)} %copy.45.sent, f32[2,8,2048]{2,1,0:T(8,128)} %pad_maximum_fusion.2.heard, bf16[4,4,512,512]{3,2,1,0:T(8,128)(2,1)} %pad_maximum_fusion.1.refs_5_.refs_6_.table), custom_call_target="tpu_custom_call" | custom-call | flops 6000000000 | bytes 25165824 | tf_op jit(solution)/shard_map/pallas_call | solution.py:410
  698.3 14.8 %shard_map.85 = f32[4,4,2,2,32,512]{5,4,3,2,1,0:T(8,128)} custom-call(f32[2,4,4,2,32,256]{5,4,3,2,1,0:T(8,128)} %bitcast.41, f32[2,32,8]{2,1,0:T(8,128)} %copy.45.sent, f32[2,8,2048]{2,1,0:T(8,128)} %pad_maximum_fusion.2.heard, bf16[4,4,512,512]{3,2,1,0:T(8,128)(2,1)} %pad_maximum_fusion.1.refs_5_.refs_6_.table, f32[4,4,2,2,32,512]{5,4,3,2,1,0:T(8,128)} %shard_map.84.rest_0_), custom_call_target="tpu_custom_call" | custom-call | flops 6000000000 | bytes 25165824 | tf_op jit(solution)/shard_map/pallas_call | solution.py:410
  713.1 64.2 %all-to-all-done.9.moved = f32[16,2,2,32,512]{4,3,2,1,0:T(8,128)} async-done(((f32[16,2,2,32,512]{4,3,2,1,0:T(8,128)}), f32[16,2,2,32,512]{4,3,2,1,0:T(8,128)}, u32[]{:S(2)}, u32[]{:S(2)}) %all-to-all-start.9) | async-done | bytes 4194336 | tf_op jit(solution)/shard_map/all_to_all | solution.py:86
  777.3 5.6 all-to-all-start.7
  782.9 1.1 collective-permute-start.1
  784.4 45.6 %collective-permute-done.1.refs_1_ = f32[2,4,256,256]{3,2,1,0:T(8,128)S(1)} collective-permute-done((f32[2,4,256,256]{3,2,1,0:T(8,128)}, f32[2,4,256,256]{3,2,1,0:T(8,128)S(1)}, u32[]{:S(2)}, u32[]{:S(2)}) %collective-permute-start.1) | collective-permute-done | bytes 2097184 | tf_op jit(solution)/shard_map/ppermute | solution.py:645
  830.1 44.9 %collective-permute-done.2.refs_3_ = f32[2,4,256,256]{3,2,1,0:T(8,128)S(1)} collective-permute-done((f32[2,4,256,256]{3,2,1,0:T(8,128)S(1)}, f32[2,4,256,256]{3,2,1,0:T(8,128)S(1)}, u32[]{:S(2)}, u32[]{:S(2)}) %collective-permute-start.2) | collective-permute-done | bytes 2097184 | tf_op jit(solution)/shard_map/ppermute | solution.py:645
  875.0 1.3 copy-done.7
  876.3 21.8 %shard_map.90 = f32[2,2,1024,512]{3,2,1,0:T(8,128)} custom-call(s32[1]{0:T(128)} %bitcast.1.place, f32[2,4,256,256]{3,2,1,0:T(8,128)} %get-tuple-element.16.refs_0_, f32[2,4,256,256]{3,2,1,0:T(8,128)} %copy-done.6, f32[2,4,256,256]{3,2,1,0:T(8,128)} %get-tuple-element.18.refs_2_, f32[2,4,256,256]{3,2,1,0:T(8,128)} %copy-done.7, ...), custom_call_target="tpu_custom_call" | custom-call | flops 6000000000 | bytes 16777216 | tf_op jit(solution)/shard_map/pallas_call | solution.py:602
  898.1 7.6 shard_map.88.rest_0_
  905.7 7.6 shard_map.89
  (39 shorter events, 3.9 us)
Async XLA Ops:
  10.1 98.6 %all-to-all-start = ((f32[16,2,2,32,512]{4,3,2,1,0:T(8,128)}), f32[16,2,2,32,512]{4,3,2,1,0:T(8,128)}, u32[]{:S(2)}, u32[]{:S(2)}) async-start(f32[16,2,2,32,512]{4,3,2,1,0:T(8,128)} %copy.33), calls=%async_computation | async-start | bytes 8388608 | tf_op jit(solution)/shard_map/all_to_all | solution.py:86
  21.6 92.2 %copy-start.8 = (f32[8]{0:T(128)S(1)}, f32[8]{0:T(128)}, u32[]{:S(2)}) copy-start(f32[8]{0:T(128)} %param.8) | copy-start | bytes 100
  108.7 97.2 %all-to-all-start.1 = ((f32[16,2,2,32,512]{4,3,2,1,0:T(8,128)}), f32[16,2,2,32,512]{4,3,2,1,0:T(8,128)}, u32[]{:S(2)}, u32[]{:S(2)}) async-start(f32[16,2,2,32,512]{4,3,2,1,0:T(8,128)} %copy.35), calls=%async_computation.1 | async-start | bytes 8388608 | tf_op jit(solution)/shard_map/all_to_all | solution.py:86
  205.9 52.4 %all-to-all-start.5 = ((f32[32,2,32,256]{3,2,1,0:T(8,128)}), f32[32,2,32,256]{3,2,1,0:T(8,128)}, u32[]{:S(2)}, u32[]{:S(2)}) async-start(f32[32,2,32,256]{3,2,1,0:T(8,128)} %bitcast.42), calls=%async_computation.5 | async-start | bytes 4194304 | tf_op jit(solution)/shard_map/all_to_all | solution.py:86
  258.3 6.5 copy-start.2
  258.3 6.6 copy-start.4
  258.3 8.3 copy-start.3
  258.3 98.8 %all-to-all-start.2 = ((f32[32,2,64,256]{3,2,1,0:T(8,128)}), f32[32,2,64,256]{3,2,1,0:T(8,128)}, u32[]{:S(2)}, u32[]{:S(2)}) async-start(f32[32,2,64,256]{3,2,1,0:T(8,128)} %bitcast.38), calls=%async_computation.2 | async-start | bytes 8388608 | tf_op jit(solution)/shard_map/all_to_all | solution.py:86
  292.0 155.3 %collective-permute-start = (f32[5,4,256,256]{3,2,1,0:T(8,128)}, f32[5,4,256,256]{3,2,1,0:T(8,128)}, u32[]{:S(2)}, u32[]{:S(2)}) collective-permute-start(f32[5,4,256,256]{3,2,1,0:T(8,128)} %get-tuple-element.12), channel_id=1, source_target_pairs={{0,16},{16,0},{1,17},{17,1},{2,18},{18,2},{3,19},{19,3},{4,20},{20... | collective-permute-start | bytes 15728648 | tf_op jit(solution)/shard_map/ppermute | solution.py:645
  357.0 115.8 %all-to-all-start.4 = ((f32[32,2,32,256]{3,2,1,0:T(8,128)}), f32[32,2,32,256]{3,2,1,0:T(8,128)}, u32[]{:S(2)}, u32[]{:S(2)}) async-start(f32[32,2,32,256]{3,2,1,0:T(8,128)} %bitcast.39), calls=%async_computation.4 | async-start | bytes 4194304 | tf_op jit(solution)/shard_map/all_to_all | solution.py:86
  472.9 52.9 %all-to-all-start.8 = ((f32[32,2,32,256]{3,2,1,0:T(8,128)}), f32[32,2,32,256]{3,2,1,0:T(8,128)S(1)}, u32[]{:S(2)}, u32[]{:S(2)}) async-start(f32[32,2,32,256]{3,2,1,0:T(8,128)} %get-tuple-element.15), calls=%async_computation.8 | async-start | bytes 4194304 | tf_op jit(solution)/shard_map/all_to_all | solution.py:86
  525.7 98.5 %copy-start = (f32[32,2,32,256]{3,2,1,0:T(8,128)}, f32[32,2,32,256]{3,2,1,0:T(8,128)S(1)}, u32[]{:S(2)}) copy-start(f32[32,2,32,256]{3,2,1,0:T(8,128)S(1)} %all-to-all-done.8) | copy-start | bytes 6291460
  624.3 52.8 %all-to-all-start.3 = ((f32[32,2,32,256]{3,2,1,0:T(8,128)}), f32[32,2,32,256]{3,2,1,0:T(8,128)S(1)}, u32[]{:S(2)}, u32[]{:S(2)}) async-start(f32[32,2,32,256]{3,2,1,0:T(8,128)} %get-tuple-element.13), calls=%async_computation.3 | async-start | bytes 4194304 | tf_op jit(solution)/shard_map/all_to_all | solution.py:86
  677.1 1.3 copy-start.1
  678.4 98.8 %all-to-all-start.9 = ((f32[16,2,2,32,512]{4,3,2,1,0:T(8,128)}), f32[16,2,2,32,512]{4,3,2,1,0:T(8,128)}, u32[]{:S(2)}, u32[]{:S(2)}) async-start(f32[16,2,2,32,512]{4,3,2,1,0:T(8,128)} %bitcast.37), calls=%async_computation.9 | async-start | bytes 8388608 | tf_op jit(solution)/shard_map/all_to_all | solution.py:86
  777.3 6.8 copy-start.5
  777.3 128.4 %all-to-all-start.7 = ((f32[16,2,2,32,512]{4,3,2,1,0:T(8,128)}), f32[16,2,2,32,512]{4,3,2,1,0:T(8,128)}, u32[]{:S(2)}, u32[]{:S(2)}) async-start(f32[16,2,2,32,512]{4,3,2,1,0:T(8,128)} %bitcast.34), calls=%async_computation.7 | async-start | bytes 8388608 | tf_op jit(solution)/shard_map/all_to_all | solution.py:86
  782.9 47.2 %collective-permute-start.1 = (f32[2,4,256,256]{3,2,1,0:T(8,128)}, f32[2,4,256,256]{3,2,1,0:T(8,128)S(1)}, u32[]{:S(2)}, u32[]{:S(2)}) collective-permute-start(f32[2,4,256,256]{3,2,1,0:T(8,128)} %get-tuple-element.17), channel_id=1, source_target_pairs={{0,16},{16,0},{1,17},{17,1},{2,18},{18,2},{3,19},{19,3},{4,20},{20... | collective-permute-start | bytes 6291464 | tf_op jit(solution)/shard_map/ppermute | solution.py:645
  784.0 91.0 %collective-permute-start.2 = (f32[2,4,256,256]{3,2,1,0:T(8,128)S(1)}, f32[2,4,256,256]{3,2,1,0:T(8,128)S(1)}, u32[]{:S(2)}, u32[]{:S(2)}) collective-permute-start(f32[2,4,256,256]{3,2,1,0:T(8,128)S(1)} %copy-done.5), channel_id=1, source_target_pairs={{0,16},{16,0},{1,17},{17,1},{2,18},{18,2},{3,19},{19,3},{4,20},{20... | collective-permute-start | bytes 6291464 | tf_op jit(solution)/shard_map/ppermute | solution.py:645
  830.1 44.9 %copy-start.6 = (f32[2,4,256,256]{3,2,1,0:T(8,128)}, f32[2,4,256,256]{3,2,1,0:T(8,128)S(1)}, u32[]{:S(2)}) copy-start(f32[2,4,256,256]{3,2,1,0:T(8,128)S(1)} %collective-permute-done.1.refs_1_) | copy-start | bytes 6291460
  875.0 1.3 copy-start.7

commit v2 on v0

--- a/solution.py
+++ b/solution.py
@@ -4,12 +4,14 @@
 import jax.numpy as jnp
 from jax import lax
 from jax.experimental import pallas as pl
+from jax.experimental.pallas import tpu as pltpu
 from jax.sharding import PartitionSpec as P
 
 depth_step = 2.0
 step_size = 0.125
 root_floor = 0.25
 radix = 4
+limit = 67043328
 
 
 def roots(wavenumber, offset, length, total):
@@ -215,6 +217,497 @@
     return (spectrum + gradient, residual)
 
 
+lanes = 128
+chunks = 2
+mesh_ids = pl.DeviceIdType.MESH
+
+
+def split(values):
+    high = values.astype(jnp.bfloat16)
+    return high, (values - high.astype(jnp.float32)).astype(jnp.bfloat16)
+
+
+def split_table(values):
+    high = lax.reduce_precision(values, 8, 7)
+    return high.astype(jnp.bfloat16), (values - high).astype(jnp.bfloat16)
+
+
+def multiply(left, right):
+    return jnp.dot(left, right, preferred_element_type=jnp.float32)
+
+
+def turned(base, high, low, left):
+    def times(values, kind):
+        return multiply(base[kind], values) if left else multiply(values, base[kind])
+
+    first = times(high, 0) + (times(high, 1) + times(low, 0))
+    second = times(high, 2) + (times(high, 3) + times(low, 2))
+    return first, second
+
+
+def moved_exactly(values, table):
+    high = values.astype(jnp.bfloat16)
+    rest = values - high.astype(jnp.float32)
+    middle = rest.astype(jnp.bfloat16)
+    low = (rest - middle.astype(jnp.float32)).astype(jnp.bfloat16)
+    return (multiply(high, table) + multiply(middle, table)) + multiply(low, table)
+
+
+def mix(parts, sign):
+    (ar, ai), (br, bi), (cr, ci), (dr, di) = parts
+    er, ei, gr, gi = ar + cr, ai + ci, ar - cr, ai - ci
+    hr, hi, kr, ki = br + dr, bi + di, sign * (br - dr), sign * (bi - di)
+    return (er + hr, ei + hi), (gr - ki, gi + kr), (er - hr, ei - hi), (gr + ki, gi - kr)
+
+
+def aligned(index, size):
+    return pl.ds(pl.multiple_of(index * size, size), size)
+
+
+def phase_of(sent, heard, f, rows, columns):
+    hr, hi = heard[0, f : f + 1, columns], heard[1, f : f + 1, columns]
+    sr, si = sent[0, rows, f : f + 1], sent[1, rows, f : f + 1]
+    return sr * hr - si * hi, sr * hi + si * hr
+
+
+def halves(first, second):
+    low = lax.broadcasted_iota(jnp.int32, first.shape, 1) < lanes // 2
+    turn = lambda x: pltpu.roll(x, lanes // 2, 1)
+    return jnp.where(low, first, turn(second)), jnp.where(low, turn(first), second)
+
+
+def whole_kernel(sizes, refs):
+    senders, hearers, layers, local, per = sizes
+    (spectrum, measured, weights, sent, heard, base, turn_row, turn_column, order, order_back) = refs[:10]
+    moved, residual, seen = refs[10:13]
+    taken, pieces, box, message, high, low, field, echo, weight = refs[13:22]
+    (in_got, in_sent, pair_got, pair_sent, back_got, back_sent, out_got, out_sent) = refs[22:30]
+    (weight_got, weight_sent, seen_got, seen_sent, load, kept, left_sent, left_got) = refs[30:]
+    groups = hearers * layers
+    devices = senders * groups
+    slab, wide = spectrum.shape[2:]
+    tall = measured.shape[2]
+    strip = wide // senders
+    rows = slab // chunks
+    spans = strip // lanes
+    width = base.shape[1]
+    planes = 2 * per
+    block = layers * rows
+    tx, rx, fq = lax.axis_index("tx"), lax.axis_index("rx"), lax.axis_index("freq")
+    mine = rx * layers + fq
+    me = tx * groups + mine
+
+    def chunk(n):
+        return pl.ds(n * rows, rows)
+
+    def remote(source, target, send, receive, device):
+        pltpu.make_async_remote_copy(
+            src_ref=source, dst_ref=target, send_sem=send, recv_sem=receive, device_id=device, device_id_type=mesh_ids
+        ).start()
+
+    def near(source, target, sem):
+        pltpu.make_async_copy(source, target, sem).start()
+
+    def settle(ref, sem):
+        pltpu.make_async_copy(ref, ref, sem).wait()
+
+    def to_group(make, send, receive):
+        def one(d, carry):
+            g = lax.rem(mine + d, groups)
+            for source, target in make(g):
+                remote(source, target, send, receive, (tx, g // layers, g % layers))
+            return carry
+
+        lax.fori_loop(1, groups, one, 0)
+        for source, target in make(mine):
+            near(source, target, receive)
+
+    def to_all(make, send, receive):
+        def one(d, carry):
+            k = lax.rem(me + d, devices)
+            source, target = make(k)
+            remote(source, target, send, receive, (k // groups, k // layers % hearers, k % layers))
+            return carry
+
+        lax.fori_loop(1, devices, one, 0)
+        source, target = make(me)
+        near(source, target, receive)
+
+    def pair_of(f, k):
+        return pl.ds((f * devices + k) * 2, 2)
+
+    def many(f):
+        return pl.ds(f * devices * 2, devices * 2)
+
+    for n in range(chunks):
+        to_group(
+            lambda g: [(spectrum.at[:, g, chunk(n), :], taken.at[rx, fq, :, chunk(n), :])], in_sent.at[n], in_got.at[n]
+        )
+    for shift in range(senders):
+        other = lax.rem(tx + shift, senders)
+        for lc in range(spans):
+            source = weights.at[:, aligned(other * spans + lc, lanes)]
+            target = weight.at[lc, aligned(tx, tall), :]
+            if shift:
+                remote(source, target, weight_sent, weight_got, (other, rx, fq))
+            else:
+                near(source, target, weight_got)
+        if shift:
+            remote(
+                measured.at[:, :, :, aligned(other, strip)],
+                seen.at[shift - 1],
+                seen_sent,
+                seen_got,
+                (other, rx, fq),
+            )
+
+    def make_pairs(f, n):
+        for g in range(layers):
+
+            def body(t, carry):
+                row, span = t // (wide // lanes), t % (wide // lanes)
+                down, across = aligned(n * (rows // 16) + row, 16), aligned(span, lanes)
+                parts = []
+                for h in range(hearers):
+                    where = aligned(h * (wide // lanes) + span, lanes)
+                    zr, zi = phase_of(sent, heard, g * local + f, down, where)
+                    ar = taken[h, layers - 1, per - 1, down, across]
+                    ai = taken[h, layers - 1, planes - 1, down, across]
+                    for j in range(layers * per - 1, -1, -1):
+                        ar, ai = ar * zr + ai * zi, ai * zr - ar * zi
+                        if j:
+                            q, d = divmod(j - 1, per)
+                            ar = ar + taken[h, q, d, down, across]
+                            ai = ai + taken[h, q, per + d, down, across]
+                    parts.append((ar, ai))
+                for s, (real, imag) in enumerate(mix(parts, 1.0)):
+                    cr, ci = turn_row[2 * s : 2 * s + 1, across], turn_row[2 * s + 1 : 2 * s + 2, across]
+                    for c, value in enumerate((real * cr - imag * ci, real * ci + imag * cr)):
+                        place = aligned((c * block + g * rows) // 16 + row, 16)
+                        high[s, place, across], low[s, place, across] = split(value)
+                return carry
+
+            lax.fori_loop(0, rows // 16 * (wide // lanes), body, 0)
+
+        def turn(s, carry):
+            first, second = turned(base, high[s, : 2 * block, :], low[s, : 2 * block, :], False)
+            field[s, :block, :] = first[:block] - second[block:]
+            field[s, block : 2 * block, :] = first[block:] + second[:block]
+            return carry
+
+        lax.fori_loop(0, radix, turn, 0)
+        for c in range(2):
+            for g in range(layers):
+                down = pl.ds(c * block + g * rows, rows)
+                for p in range(hearers):
+                    across = pl.ds(p * lanes, lanes)
+                    for lc in range(spans):
+                        values = halves(field[2 * lc, down, across], field[2 * lc + 1, down, across])
+                        for k in range(senders):
+                            place = (f * devices + (k * hearers + p) * layers + g) * 2 + c
+                            message[place, chunk(n), lc * lanes : (lc + 1) * lanes] = values[k]
+
+    def send_pairs(f, n):
+        to_all(
+            lambda k: (message.at[pair_of(f, k), chunk(n), :], box.at[pair_of(f, me), chunk(n), :]),
+            pair_sent.at[f, n],
+            pair_got.at[f, n],
+        )
+
+    def load_echo(f):
+        for c in range(2):
+            for lc in range(spans):
+                for shift in range(senders):
+                    source = (
+                        seen.at[shift - 1, c, f, :, pl.ds(lc * lanes, lanes)]
+                        if shift
+                        else measured.at[c, f, :, aligned(tx * spans + lc, lanes)]
+                    )
+                    other = lax.rem(tx + senders - shift, senders)
+                    near(source, echo.at[c, lc, aligned(other, tall), :], load)
+        settle(echo, load)
+
+    def send_left(f):
+        for c in range(2):
+            for lc in range(spans):
+                for shift in range(senders):
+                    other = lax.rem(tx + senders - shift, senders)
+                    source = echo.at[c, lc, aligned(other, tall), :]
+                    target = residual.at[c, f, :, aligned(tx * spans + lc, lanes)]
+                    if shift:
+                        remote(source, target, left_sent, left_got.at[f], (other, rx, fq))
+                    else:
+                        near(source, target, kept)
+
+    def settle_left():
+        settle(echo.at[:, :, pl.ds(0, tall), :], kept)
+        if senders > 1:
+            settle(echo.at[:, :, pl.ds(tall, tall * (senders - 1)), :], left_sent)
+
+    quarter = devices // radix
+
+    def columns(f):
+        def gather(t, carry):
+            d, row = t // (slab // 16), t % (slab // 16)
+            here, down = aligned(row, 16), aligned(t, 16)
+            for lc in range(spans):
+                across = slice(lc * lanes, (lc + 1) * lanes)
+                parts = [
+                    tuple(box[(f * devices + q * quarter + d) * 2 + c, here, across] for c in range(2))
+                    for q in range(radix)
+                ]
+                for s, (real, imag) in enumerate(mix(parts, 1.0)):
+                    cr, ci = turn_column[2 * s, down, :], turn_column[2 * s + 1, down, :]
+                    for c, value in enumerate((real * cr - imag * ci, real * ci + imag * cr)):
+                        place = slice(c * strip + lc * lanes, c * strip + (lc + 1) * lanes)
+                        high[s, down, place], low[s, down, place] = split(value)
+            return carry
+
+        lax.fori_loop(0, width // 16, gather, 0)
+
+        def middle(s, carry):
+            first, second = turned(base, high[s], low[s], True)
+            picked = pl.ds(s, width, stride=radix)
+            for c in range(2):
+                if c:
+                    value = first[:, strip:] + second[:, :strip]
+                else:
+                    value = first[:, :strip] - second[:, strip:]
+                value = moved_exactly(value, order_back[...])
+                left = []
+                for lc in range(spans):
+                    across = slice(lc * lanes, (lc + 1) * lanes)
+                    part = weight[lc, picked, :] * (echo[c, lc, picked, :] - value[:, across])
+                    echo[c, lc, picked, :] = part
+                    left.append(part)
+                parts = split(jnp.concatenate(left, axis=1))
+                for ref, part in zip((high, low), parts):
+                    ref[s, :, c * strip : (c + 1) * strip] = multiply(part, order[...]).astype(jnp.bfloat16)
+            first, second = turned(base, high[s], low[s], True)
+            field[s, :, :strip] = first[:, :strip] + second[:, strip:]
+            field[s, :, strip:] = first[:, strip:] - second[:, :strip]
+            return carry
+
+        lax.fori_loop(0, radix, middle, 0)
+
+        def scatter(t, carry):
+            d, row = t // (slab // 16), t % (slab // 16)
+            here, down = aligned(row, 16), aligned(t, 16)
+            for lc in range(spans):
+                across = slice(lc * lanes, (lc + 1) * lanes)
+                parts = []
+                for s in range(radix):
+                    real = field[s, down, lc * lanes : (lc + 1) * lanes]
+                    imag = field[s, down, strip + lc * lanes : strip + (lc + 1) * lanes]
+                    cr, ci = turn_column[2 * s, down, :], turn_column[2 * s + 1, down, :]
+                    parts.append((real * cr + imag * ci, imag * cr - real * ci))
+                for q, values in enumerate(mix(parts, -1.0)):
+                    for c in range(2):
+                        message[(f * devices + q * quarter + d) * 2 + c, here, across] = values[c]
+            return carry
+
+        lax.fori_loop(0, width // 16, scatter, 0)
+
+    def send_back(f, n):
+        to_all(
+            lambda k: (message.at[pair_of(f, k), chunk(n), :], pieces.at[pair_of(f, me), chunk(n), :]),
+            back_sent.at[f, n],
+            back_got.at[f, n],
+        )
+
+    def gradient(f, n):
+        for c in range(2):
+            for g in range(layers):
+                down = pl.ds(c * block + g * rows, rows)
+                for p in range(hearers):
+                    for lc in range(spans):
+                        across = slice(lc * lanes, (lc + 1) * lanes)
+                        where = [(f * devices + (k * hearers + p) * layers + g) * 2 + c for k in range(senders)]
+                        values = halves(*[pieces[k, chunk(n), across] for k in where])
+                        for k in range(2):
+                            spot = (2 * lc + k, down, pl.ds(p * lanes, lanes))
+                            high[spot], low[spot] = split(values[k])
+
+        def turn(s, carry):
+            first, second = turned(base, high[s, : 2 * block, :], low[s, : 2 * block, :], False)
+            field[s, :block, :] = first[:block] + second[block:]
+            field[s, block : 2 * block, :] = first[block:] - second[:block]
+            return carry
+
+        lax.fori_loop(0, radix, turn, 0)
+
+        def body(t, carry):
+            row, span = t // (wide // lanes), t % (wide // lanes)
+            across = aligned(span, lanes)
+            for g in range(layers):
+                spots = [aligned((c * block + g * rows) // 8 + row, 8) for c in range(2)]
+                parts = []
+                for s in range(radix):
+                    real, imag = field[s, spots[0], across], field[s, spots[1], across]
+                    cr, ci = turn_row[2 * s : 2 * s + 1, across], turn_row[2 * s + 1 : 2 * s + 2, across]
+                    parts.append((real * cr + imag * ci, imag * cr - real * ci))
+                for h, values in enumerate(mix(parts, -1.0)):
+                    for c in range(2):
+                        field[h, spots[c], across] = step_size * values[c]
+            here = aligned(n * (rows // 8) + row, 8)
+            inner = aligned(span % spans, lanes)
+            for h in range(hearers):
+                sums = [None] * (layers * per)
+                for g in range(layers):
+                    where = aligned(h * (wide // lanes) + span, lanes)
+                    zr, zi = phase_of(sent, heard, g * local + f, here, where)
+                    tr, ti = [field[h, aligned((c * block + g * rows) // 8 + row, 8), across] for c in range(2)]
+                    for j in range(layers * per):
+                        tr, ti = tr * zr - ti * zi, tr * zi + ti * zr
+                        sums[j] = (sums[j][0] + tr, sums[j][1] + ti) if g else (tr, ti)
+                for j in range(layers * per):
+                    q, d = divmod(j, per)
+                    for c in range(2):
+                        place = ((h * layers + q) * senders + span // spans) * planes + c * per + d
+                        value = sums[j][c]
+                        if f:
+                            value = value + box[place, here, inner]
+                        box[place, here, inner] = value
+            return carry
+
+        lax.fori_loop(0, rows // 8 * (wide // lanes), body, 0)
+
+    def send_out(n):
+        to_group(
+            lambda g: [
+                (
+                    box.at[pl.ds((g * senders + k) * planes, planes), chunk(n), :],
+                    moved.at[:, mine, chunk(n), pl.ds(k * strip, strip)],
+                )
+                for k in range(senders)
+            ],
+            out_sent.at[n],
+            out_got.at[n],
+        )
+
+    for n in range(chunks):
+        settle(taken.at[:, :, :, chunk(n), :], in_got.at[n])
+        make_pairs(0, n)
+        send_pairs(0, n)
+        if n:
+            for k in range(n):
+                for f in range(1, local):
+                    send_pairs(f, k)
+        for f in range(1, local):
+            make_pairs(f, n)
+    for f in range(1, local):
+        send_pairs(f, chunks - 1)
+    settle(weight, weight_got)
+    settle(seen, seen_got)
+    for f in range(local):
+        if f:
+            settle_left()
+        load_echo(f)
+        for n in range(chunks):
+            settle(box.at[many(f), chunk(n), :], pair_got.at[f, n])
+            settle(message.at[pl.ds(0, (devices - 1) * 2), chunk(n), :], pair_sent.at[f, n])
+        columns(f)
+        for n in range(chunks):
+            send_back(f, n)
+        send_left(f)
+    for f in range(local):
+        for n in range(chunks):
+            settle(pieces.at[many(f), chunk(n), :], back_got.at[f, n])
+            gradient(f, n)
+            if f == local - 1:
+                send_out(n)
+    settle_left()
+    for n in range(chunks):
+        settle(spectrum.at[:, pl.ds(0, groups - 1), chunk(n), :], in_sent.at[n])
+        for f in range(local):
+            settle(message.at[pl.ds(0, (devices - 1) * 2), chunk(n), :], back_sent.at[f, n])
+        settle(box.at[pl.ds(0, (groups - 1) * senders * planes), chunk(n), :], out_sent.at[n])
+        settle(moved.at[:, :, chunk(n), :], out_got.at[n])
+    settle(weights.at[:, pl.ds(0, strip * (senders - 1))], weight_sent)
+    settle(seen, seen_sent)
+    for f in range(local):
+        settle(residual.at[:, f, :, pl.ds(0, strip * (senders - 1))], left_got.at[f])
+
+
+def per_device_whole(spectrum, measured, wavenumber, send_weight, hear_weight, aperture):
+    _, per, rows_sent, rows_heard = spectrum.shape
+    local = measured.shape[1]
+    senders = lax.axis_size("tx")
+    hearers = lax.axis_size("rx")
+    layers = lax.axis_size("freq")
+    total = rows_sent * senders
+    groups = hearers * layers
+    slab = rows_sent // groups
+    strip = rows_heard // senders
+    width = total // radix
+
+    first_row = lax.axis_index("tx") * rows_sent + (lax.axis_index("rx") * layers + lax.axis_index("freq")) * slab
+    sent_phase = depth_step * roots(wavenumber, first_row, slab, total).T
+    heard_phase = depth_step * roots(wavenumber, 0, total, total)
+    sent = jnp.stack([jnp.cos(sent_phase), jnp.sin(sent_phase)])
+    heard = jnp.stack([jnp.cos(heard_phase), jnp.sin(heard_phase)])
+    cosine, sine = unit_pair(width, width, width)
+    base = jnp.stack(split_table(cosine) + split_table(sine))
+    turn = jnp.stack(unit_pair(radix, width, total), axis=1).reshape(2 * radix, width) / math.sqrt(total)
+    turn_column = jnp.broadcast_to(turn[:, :, None], (2 * radix, width, lanes))
+
+    place = jnp.arange(strip, dtype=jnp.int32)
+    source = place % (strip // radix) * radix + place // (strip // radix)
+    order = (place[:, None] == source[None, :]).astype(jnp.bfloat16)
+    tiles_sent, tiles_heard = aperture.shape
+    gate = jnp.repeat(aperture.astype(jnp.float32), rows_heard // tiles_heard, axis=1) * hear_weight[None, :]
+    weights = gate[:, None, :] * send_weight.reshape(tiles_sent, -1)[:, :, None]
+    weights = weights.reshape(rows_sent, rows_heard)
+
+    sizes = (senders, hearers, layers, local, per)
+    anywhere = pl.BlockSpec(memory_space=pl.ANY)
+    inside = pl.BlockSpec(memory_space=pltpu.VMEM)
+    count = local * senders * groups * 2
+    blocks = spectrum.reshape(2 * per, groups, slab, rows_heard)
+    floats = lambda *shape: pltpu.VMEM(shape, jnp.float32)
+    sems = pltpu.SemaphoreType.DMA
+    moved, residual, _ = pl.pallas_call(
+        lambda *refs: whole_kernel(sizes, refs),
+        in_specs=[anywhere] * 3 + [inside] * 7,
+        out_specs=[anywhere] * 3,
+        out_shape=[
+            jax.ShapeDtypeStruct(blocks.shape, jnp.float32),
+            jax.ShapeDtypeStruct(measured.shape, jnp.float32),
+            jax.ShapeDtypeStruct((senders - 1, 2, local, rows_sent, strip), jnp.float32),
+        ],
+        scratch_shapes=[
+            floats(hearers, layers, 2 * per, slab, rows_heard),
+            floats(count, slab, strip),
+            floats(count, slab, strip),
+            floats(count, slab, strip),
+            pltpu.VMEM((radix, width, width), jnp.bfloat16),
+            pltpu.VMEM((radix, width, width), jnp.bfloat16),
+            floats(radix, width, width),
+            floats(2, strip // lanes, total, lanes),
+            floats(strip // lanes, total, lanes),
+        ]
+        + [sems((chunks,))] * 2
+        + [sems((local, chunks))] * 4
+        + [sems((chunks,))] * 2
+        + [sems] * 7
+        + [sems((local,))],
+        compiler_params=pltpu.CompilerParams(vmem_limit_bytes=limit, has_side_effects=True),
+    )(blocks, measured, weights, sent, heard, base, turn, turn_column, order, order.T)
+    return ((blocks + moved).reshape(spectrum.shape), residual)
+
+
+def fits(mesh, sent, heard):
+    senders, hearers, layers = [mesh.shape[axis] for axis in ("tx", "rx", "freq")]
+    rows = sent // senders // (hearers * layers)
+    return (
+        hearers == radix
+        and senders == 2
+        and sent == heard
+        and rows % (16 * chunks) == 0
+        and heard // hearers // radix == lanes
+    )
+
+
 def solution(mesh):
     placed = (
         P(None, "freq", "tx", "rx"),
@@ -224,8 +717,13 @@
         P("rx"),
         P("tx", "rx"),
     )
+
+    def body(*args):
+        sent, heard = args[3].shape[0] * mesh.shape["tx"], args[4].shape[0] * mesh.shape["rx"]
+        return (per_device_whole if fits(mesh, sent, heard) else per_device)(*args)
+
     return jax.shard_map(
-        per_device,
+        body,
         mesh=mesh,
         in_specs=placed,
         out_specs=(P(None, "freq", "tx", "rx"), P(None, "freq", "tx", "rx")),

time: 1460 us -> 795 us (0.54)
  blocking collectives: 752 us -> 0 us
  Pallas kernels: 49.4 us -> 747 us
  waiting for transfers between devices: 330 us -> 0 us
  local copies, waits for them, and re-layouts: 156 us -> 10.6 us
  matrix products: 57.7 us -> 0 us
  other arithmetic: 73.9 us -> 28.3 us
  starting transfers between devices: 20.2 us -> 0 us
    all_to_all x5 -> x0, blocking collectives: 752 us -> none  [exchange(): return lax.all_to_all(values, axes, split_axis=0, concat_axis=0, tiled=True)]
    pallas_call x2 -> x1, Pallas kernels: 49.4 us -> 747 us  [per_device_whole(): pl.pallas_call(lambda *refs: whole_kernel(sizes, refs), in_specs=[anywher...]
    all_to_all x3 -> x0, waiting for transfers between devices: 330 us -> none  [exchange(): return lax.all_to_all(values, axes, split_axis=0, concat_axis=0, tiled=True)]
    transpose x12 -> x0, local copies, waits for them, and re-layouts: 87.3 us -> none  [the longest x4 38.8 us: unmix(): jnp.transpose(done, (2, 1, 0, 3, 4))]
    dot_general x8 -> x0, matrix products: 57.7 us -> none  [the longest x4 28.9 us: dft(): second = jnp.einsum(form, sine, mixed, precision=lax.Precision.HIGH)]
    reshape x4 -> x0, local copies, waits for them, and re-layouts: 30.9 us -> none  [the longest x1 11.6 us: per_device(): jnp.transpose(done, (2, 1, 3, 4, 0, 5))]
    mul x3 -> x1, local copies, waits for them, and re-layouts: 23.5 us -> 0.11 us  [per_device_whole(): jnp.repeat(aperture.astype(jnp.float32), rows_heard // tiles_heard, axis=1)]
    all_to_all x3 -> x0, starting transfers between devices: 20.2 us -> none  [exchange(): return lax.all_to_all(values, axes, split_axis=0, concat_axis=0, tiled=True)]
  transfers between devices with their start and end apart: 3 -> 0, of which waited for: 3 -> 0; matrix products, arithmetic and copies ran while one was open for 2% -> 0% of each run, Pallas kernels for 0% -> 0%
where the time goes in v2:
time: 795 us; the launch traced here: 786 us
  Pallas kernels  747 us (94%)
  other arithmetic  28.3 us (4%)
  local copies, waits for them, and re-layouts  10.6 us (1%)
    pallas_call x1, Pallas kernels, per_device_whole(): pl.pallas_call(lambda *refs: whole_kernel(sizes, refs), in_specs=[anywher...  747 us

profile of v2, /device:TPU:19, one launch (start us, length us, event | category | flops | bytes accessed | tf_op | source)
XLA Modules:
  0.0 786.1 jit_solution(14031269189765628155)
XLA Ops:
  0.7 0.7 mul.257
  1.4 0.1 fusion.23
  1.5 0.7 convert_element_type.106
  2.3 0.1 fusion.20
  2.4 0.0 copy-start
  2.4 0.7 copy.14.refs_3_
  3.1 0.3 fusion.13
  3.5 0.7 pad_maximum_fusion.1.refs_4_
  4.2 0.8 bitcast_multiply_fusion.1
  5.0 0.1 copy.12
  5.1 0.8 fusion.11
  5.8 4.5 fusion
  10.3 4.3 reduce-precision_convert_fusion
  14.6 0.0 copy-start.1
  14.6 1.6 pad_maximum_fusion.refs_5_
  16.2 0.0 copy-done.1
  16.2 1.5 bitcast_multiply_fusion.refs_2_
  17.8 0.0 copy-done
  17.8 1.9 broadcast_in_dim.5.refs_7_
  19.7 746.6 %shard_map.77 = (f32[4,16,64,512]{3,2,1,0:T(8,128)}, f32[2,2,1024,512]{3,2,1,0:T(8,128)}, f32[1,2,2,1024,256]{4,3,2,1,0:T(8,128)}) custom-call(f32[4,16,64,512]{3,2,1,0:T(8,128)} %bitcast.6, f32[2,2,1024,512]{3,2,1,0:T(8,128)} %refs_1_.1, f32[1024,512]{1,0:T(8,128)} %bitcast_multiply_fusion.refs_2_, f32[2,64,8]{2,1,0:T(8,128)} %copy.14.refs_3_, ...), custom_call_target="tpu_custom_call" | custom-call | tf_op jit(solution)/shard_map/pallas_call | solution.py:669
  766.3 12.1 %add.152 = f32[4,16,64,512]{3,2,1,0:T(8,128)} add(f32[4,16,64,512]{3,2,1,0:T(8,128)} %bitcast.7, f32[4,16,64,512]{3,2,1,0:T(8,128)} %get-tuple-element.4) | non-fusion elementwise | flops 2097152 | bytes 25165824 | tf_op jit(solution)/shard_map/add | solution.py:696
  778.4 7.8 copy.16
  (7 shorter events, 0.1 us)
Async XLA Ops:
  2.4 15.3 %copy-start = (f32[8,512]{1,0:T(8,128)}, f32[8,512]{1,0:T(8,128)S(1)}, u32[]{:S(2)}) copy-start(f32[8,512]{1,0:T(8,128)S(1)} %div.20.refs_6_) | copy-start | bytes 49156
  14.6 1.6 copy-start.1

commit v3 on v2

--- a/solution.py
+++ b/solution.py
@@ -227,11 +227,6 @@
     return high, (values - high.astype(jnp.float32)).astype(jnp.bfloat16)
 
 
-def split_table(values):
-    high = lax.reduce_precision(values, 8, 7)
-    return high.astype(jnp.bfloat16), (values - high).astype(jnp.bfloat16)
-
-
 def multiply(left, right):
     return jnp.dot(left, right, preferred_element_type=jnp.float32)
 
@@ -278,11 +273,12 @@
 
 def whole_kernel(sizes, refs):
     senders, hearers, layers, local, per = sizes
-    (spectrum, measured, weights, sent, heard, base, turn_row, turn_column, order, order_back) = refs[:10]
-    moved, residual, seen = refs[10:13]
-    taken, pieces, box, message, high, low, field, echo, weight = refs[13:22]
-    (in_got, in_sent, pair_got, pair_sent, back_got, back_sent, out_got, out_sent) = refs[22:30]
-    (weight_got, weight_sent, seen_got, seen_sent, load, kept, left_sent, left_got) = refs[30:]
+    spectrum, measured, weights, wavenumber = refs[:4]
+    moved, residual, seen = refs[4:7]
+    taken, pieces, box, message, high, low, field, echo, weight = refs[7:16]
+    sent, heard, base, turn_row, turn_column, order, order_back = refs[16:23]
+    (in_got, in_sent, pair_got, pair_sent, back_got, back_sent, out_got, out_sent) = refs[23:31]
+    (weight_got, weight_sent, seen_got, seen_sent, load, kept, left_sent, left_got) = refs[31:]
     groups = hearers * layers
     devices = senders * groups
     slab, wide = spectrum.shape[2:]
@@ -290,7 +286,7 @@
     strip = wide // senders
     rows = slab // chunks
     spans = strip // lanes
-    width = base.shape[1]
+    width = high.shape[1]
     planes = 2 * per
     block = layers * rows
     tx, rx, fq = lax.axis_index("tx"), lax.axis_index("rx"), lax.axis_index("freq")
@@ -312,24 +308,43 @@
         pltpu.make_async_copy(ref, ref, sem).wait()
 
     def to_group(make, send, receive):
-        def one(d, carry):
-            g = lax.rem(mine + d, groups)
-            for source, target in make(g):
-                remote(source, target, send, receive, (tx, g // layers, g % layers))
-            return carry
-
-        lax.fori_loop(1, groups, one, 0)
+        def far(d, carry):
+            j = lax.rem(fq + d, layers)
+            for there in ((rx + 2) % hearers, 3 - rx, rx + 1 - 2 * (rx % 2)):
+                for source, target in make(there * layers + j):
+                    remote(source, target, send, receive, (tx, there, j))
+            return carry
+
+        def close(d, carry):
+            j = lax.rem(fq + d, layers)
+            for source, target in make(rx * layers + j):
+                remote(source, target, send, receive, (tx, rx, j))
+            return carry
+
+        lax.fori_loop(0, layers, far, 0)
+        lax.fori_loop(1, layers, close, 0)
         for source, target in make(mine):
             near(source, target, receive)
 
     def to_all(make, send, receive):
-        def one(d, carry):
-            k = lax.rem(me + d, devices)
-            source, target = make(k)
-            remote(source, target, send, receive, (k // groups, k // layers % hearers, k % layers))
-            return carry
-
-        lax.fori_loop(1, devices, one, 0)
+        def place(j, there):
+            return (j // layers * hearers + there) * layers + j % layers
+
+        def far(d, carry):
+            j = lax.rem(tx * layers + fq + d, senders * layers)
+            for there in ((rx + 2) % hearers, 3 - rx, rx + 1 - 2 * (rx % 2)):
+                source, target = make(place(j, there))
+                remote(source, target, send, receive, (j // layers, there, j % layers))
+            return carry
+
+        def close(d, carry):
+            j = lax.rem(tx * layers + fq + d, senders * layers)
+            source, target = make(place(j, rx))
+            remote(source, target, send, receive, (j // layers, rx, j % layers))
+            return carry
+
+        lax.fori_loop(0, senders * layers, far, 0)
+        lax.fori_loop(1, senders * layers, close, 0)
         source, target = make(me)
         near(source, target, receive)
 
@@ -360,6 +375,56 @@
                 seen_got,
                 (other, rx, fq),
             )
+
+    total = width * radix
+
+    def make_phases(ref, numbers, offset, axis, shape):
+        indices = offset + lax.broadcasted_iota(jnp.int32, shape, axis)
+        signed = jnp.where(indices < total // 2, indices, indices - total)
+        waves = 2.0 * jnp.pi / total * signed.astype(jnp.float32)
+        phase = depth_step * jnp.sqrt(jnp.maximum(numbers * numbers - waves * waves, 0.0) + root_floor)
+        ref[0], ref[1] = jnp.cos(phase), jnp.sin(phase)
+
+    def make_tables():
+        numbers = wavenumber[...]
+        freqs = numbers.shape[1]
+        square = (freqs, freqs)
+        same = lax.broadcasted_iota(jnp.int32, square, 0) == lax.broadcasted_iota(jnp.int32, square, 1)
+        tall_numbers = jnp.sum(jnp.where(same, jnp.broadcast_to(numbers, square), 0.0), axis=1, keepdims=True)
+        make_phases(sent, numbers, tx * tall + mine * slab, 0, (slab, freqs))
+        make_phases(heard, tall_numbers, 0, 1, (freqs, total))
+        scale = 1.0 / math.sqrt(total)
+
+        def angles(product, period):
+            return 2.0 * math.pi / period * product.astype(jnp.float32)
+
+        def fill(t, carry):
+            down = aligned(t, 16)
+            row = t * 16 + lax.broadcasted_iota(jnp.int32, (16, width), 0)
+            product = jnp.bitwise_and(row * lax.broadcasted_iota(jnp.int32, (16, width), 1), width - 1)
+            phase = angles(product, width)
+            for k, values in enumerate((jnp.cos(phase), jnp.sin(phase))):
+                base[2 * k, down, :], base[2 * k + 1, down, :] = split(values)
+            row = row[:, :lanes]
+            for s in range(radix):
+                phase = angles(s * row, total)
+                turn_column[2 * s, down, :] = jnp.cos(phase) * scale
+                turn_column[2 * s + 1, down, :] = jnp.sin(phase) * scale
+            return carry
+
+        lax.fori_loop(0, width // 16, fill, 0)
+        for s in range(radix):
+            phase = angles(s * lax.broadcasted_iota(jnp.int32, (1, width), 1), total)
+            turn_row[2 * s : 2 * s + 1, :] = jnp.cos(phase) * scale
+            turn_row[2 * s + 1 : 2 * s + 2, :] = jnp.sin(phase) * scale
+        part = strip // radix
+        for ref, axis in ((order, 0), (order_back, 1)):
+            natural = lax.broadcasted_iota(jnp.int32, (strip, strip), axis)
+            place = lax.broadcasted_iota(jnp.int32, (strip, strip), 1 - axis)
+            source = jnp.bitwise_and(place, part - 1) * radix + place // part
+            ref[...] = jnp.where(natural == source, 1.0, 0.0).astype(jnp.bfloat16)
+
+    make_tables()
 
     def make_pairs(f, n):
         for g in range(layers):
@@ -424,25 +489,23 @@
                         else measured.at[c, f, :, aligned(tx * spans + lc, lanes)]
                     )
                     other = lax.rem(tx + senders - shift, senders)
-                    near(source, echo.at[c, lc, aligned(other, tall), :], load)
-        settle(echo, load)
+                    near(source, echo.at[f, c, lc, aligned(other, tall), :], load.at[f])
 
     def send_left(f):
         for c in range(2):
             for lc in range(spans):
                 for shift in range(senders):
                     other = lax.rem(tx + senders - shift, senders)
-                    source = echo.at[c, lc, aligned(other, tall), :]
+                    source = echo.at[f, c, lc, aligned(other, tall), :]
                     target = residual.at[c, f, :, aligned(tx * spans + lc, lanes)]
                     if shift:
-                        remote(source, target, left_sent, left_got.at[f], (other, rx, fq))
+                        remote(source, target, left_sent.at[f], left_got.at[f], (other, rx, fq))
                     else:
-                        near(source, target, kept)
-
-    def settle_left():
-        settle(echo.at[:, :, pl.ds(0, tall), :], kept)
-        if senders > 1:
-            settle(echo.at[:, :, pl.ds(tall, tall * (senders - 1)), :], left_sent)
+                        near(source, target, kept.at[f])
+
+    def settle_left(f):
+        settle(echo.at[f, :, :, pl.ds(0, tall), :], kept.at[f])
+        settle(echo.at[f, :, :, pl.ds(tall, tall * (senders - 1)), :], left_sent.at[f])
 
     quarter = devices // radix
 
@@ -477,8 +540,8 @@
                 left = []
                 for lc in range(spans):
                     across = slice(lc * lanes, (lc + 1) * lanes)
-                    part = weight[lc, picked, :] * (echo[c, lc, picked, :] - value[:, across])
-                    echo[c, lc, picked, :] = part
+                    part = weight[lc, picked, :] * (echo[f, c, lc, picked, :] - value[:, across])
+                    echo[f, c, lc, picked, :] = part
                     left.append(part)
                 parts = split(jnp.concatenate(left, axis=1))
                 for ref, part in zip((high, low), parts):
@@ -600,15 +663,16 @@
     settle(weight, weight_got)
     settle(seen, seen_got)
     for f in range(local):
-        if f:
-            settle_left()
         load_echo(f)
+    for f in range(local):
+        settle(echo.at[f], load.at[f])
         for n in range(chunks):
             settle(box.at[many(f), chunk(n), :], pair_got.at[f, n])
             settle(message.at[pl.ds(0, (devices - 1) * 2), chunk(n), :], pair_sent.at[f, n])
         columns(f)
         for n in range(chunks):
             send_back(f, n)
+    for f in range(local):
         send_left(f)
     for f in range(local):
         for n in range(chunks):
@@ -616,7 +680,8 @@
             gradient(f, n)
             if f == local - 1:
                 send_out(n)
-    settle_left()
+    for f in range(local):
+        settle_left(f)
     for n in range(chunks):
         settle(spectrum.at[:, pl.ds(0, groups - 1), chunk(n), :], in_sent.at[n])
         for f in range(local):
@@ -641,19 +706,6 @@
     strip = rows_heard // senders
     width = total // radix
 
-    first_row = lax.axis_index("tx") * rows_sent + (lax.axis_index("rx") * layers + lax.axis_index("freq")) * slab
-    sent_phase = depth_step * roots(wavenumber, first_row, slab, total).T
-    heard_phase = depth_step * roots(wavenumber, 0, total, total)
-    sent = jnp.stack([jnp.cos(sent_phase), jnp.sin(sent_phase)])
-    heard = jnp.stack([jnp.cos(heard_phase), jnp.sin(heard_phase)])
-    cosine, sine = unit_pair(width, width, width)
-    base = jnp.stack(split_table(cosine) + split_table(sine))
-    turn = jnp.stack(unit_pair(radix, width, total), axis=1).reshape(2 * radix, width) / math.sqrt(total)
-    turn_column = jnp.broadcast_to(turn[:, :, None], (2 * radix, width, lanes))
-
-    place = jnp.arange(strip, dtype=jnp.int32)
-    source = place % (strip // radix) * radix + place // (strip // radix)
-    order = (place[:, None] == source[None, :]).astype(jnp.bfloat16)
     tiles_sent, tiles_heard = aperture.shape
     gate = jnp.repeat(aperture.astype(jnp.float32), rows_heard // tiles_heard, axis=1) * hear_weight[None, :]
     weights = gate[:, None, :] * send_weight.reshape(tiles_sent, -1)[:, :, None]
@@ -663,12 +715,13 @@
     anywhere = pl.BlockSpec(memory_space=pl.ANY)
     inside = pl.BlockSpec(memory_space=pltpu.VMEM)
     count = local * senders * groups * 2
+    freqs = local * layers
     blocks = spectrum.reshape(2 * per, groups, slab, rows_heard)
     floats = lambda *shape: pltpu.VMEM(shape, jnp.float32)
     sems = pltpu.SemaphoreType.DMA
     moved, residual, _ = pl.pallas_call(
         lambda *refs: whole_kernel(sizes, refs),
-        in_specs=[anywhere] * 3 + [inside] * 7,
+        in_specs=[anywhere] * 3 + [inside],
         out_specs=[anywhere] * 3,
         out_shape=[
             jax.ShapeDtypeStruct(blocks.shape, jnp.float32),
@@ -683,16 +736,23 @@
             pltpu.VMEM((radix, width, width), jnp.bfloat16),
             pltpu.VMEM((radix, width, width), jnp.bfloat16),
             floats(radix, width, width),
-            floats(2, strip // lanes, total, lanes),
+            floats(local, 2, strip // lanes, total, lanes),
             floats(strip // lanes, total, lanes),
+            floats(2, slab, freqs),
+            floats(2, freqs, total),
+            pltpu.VMEM((4, width, width), jnp.bfloat16),
+            floats(2 * radix, width),
+            floats(2 * radix, width, lanes),
+            pltpu.VMEM((strip, strip), jnp.bfloat16),
+            pltpu.VMEM((strip, strip), jnp.bfloat16),
         ]
         + [sems((chunks,))] * 2
         + [sems((local, chunks))] * 4
         + [sems((chunks,))] * 2
-        + [sems] * 7
-        + [sems((local,))],
+        + [sems] * 4
+        + [sems((local,))] * 4,
         compiler_params=pltpu.CompilerParams(vmem_limit_bytes=limit, has_side_effects=True),
-    )(blocks, measured, weights, sent, heard, base, turn, turn_column, order, order.T)
+    )(blocks, measured, weights, wavenumber.reshape(1, -1))
     return ((blocks + moved).reshape(spectrum.shape), residual)
 
 
@@ -705,6 +765,7 @@
         and sent == heard
         and rows % (16 * chunks) == 0
         and heard // hearers // radix == lanes
+        and heard & (heard - 1) == 0
     )
 
 

time: 795 us -> 762 us (0.958); the launches traced: 786 us -> 762 us
  other arithmetic: 28.3 us -> 15.9 us
  Pallas kernels: 747 us -> 737 us
    convert_element_type x3 -> x0, other arithmetic: 9.52 us -> none  [the longest x2 8.77 us: split_table(): return (high.astype(jnp.bfloat16), (values - high).astype(jnp.bfloat16))]
    pallas_call x1, Pallas kernels: 747 us -> 737 us  [per_device_whole(): pl.pallas_call(lambda *refs: whole_kernel(sizes, refs), in_specs=[anywher...]
where the time goes in v3:
time: 762 us
  Pallas kernels  737 us (97%)
  other arithmetic  15.9 us (2%)
  local copies, waits for them, and re-layouts  7.87 us (1%)
    pallas_call x1, Pallas kernels, per_device_whole(): pl.pallas_call(lambda *refs: whole_kernel(sizes, refs), in_specs=[anywher...  737 us

profile of v3, /device:TPU:19, one launch (start us, length us, event | category | flops | bytes accessed | tf_op | source)
XLA Modules:
  0.0 761.5 jit_solution(7338464456076805944)
XLA Ops:
  0.6 0.7 convert_element_type.3
  1.4 0.8 bitcast_multiply_fusion.1
  2.2 0.1 copy.9
  2.3 2.2 bitcast_multiply_fusion.refs_2_
  4.5 737.1 %shard_map.77 = (f32[4,16,64,512]{3,2,1,0:T(8,128)}, f32[2,2,1024,512]{3,2,1,0:T(8,128)}, f32[1,2,2,1024,256]{4,3,2,1,0:T(8,128)}) custom-call(f32[4,16,64,512]{3,2,1,0:T(8,128)} %bitcast.7, f32[2,2,1024,512]{3,2,1,0:T(8,128)} %refs_1_.1, f32[1024,512]{1,0:T(8,128)} %bitcast_multiply_fusion.refs_2_, f32[1,8]{1,0:T(1,128)} %bitcast.10), custom_call_target="tpu_custom_call" | custom-call | tf_op jit(solution)/shard_map/pallas_call | solution.py:722
  741.6 12.1 %add.3 = f32[4,16,64,512]{3,2,1,0:T(8,128)} add(f32[4,16,64,512]{3,2,1,0:T(8,128)} %bitcast.8, f32[4,16,64,512]{3,2,1,0:T(8,128)} %get-tuple-element.4) | non-fusion elementwise | flops 2097152 | bytes 25165824 | tf_op jit(solution)/shard_map/add | solution.py:756
  753.8 7.8 %copy.11 = f32[2,2,1024,512]{3,2,1,0:T(8,128)} copy(f32[2,2,1024,512]{3,2,1,0:T(8,128)} %get-tuple-element.9) | data formatting | bytes 16777216

commit v4 on v3

--- a/solution.py
+++ b/solution.py
@@ -11,7 +11,7 @@
 step_size = 0.125
 root_floor = 0.25
 radix = 4
-limit = 67043328
+limit = 54 << 20
 
 
 def roots(wavenumber, offset, length, total):
@@ -275,10 +275,10 @@
     senders, hearers, layers, local, per = sizes
     spectrum, measured, weights, wavenumber = refs[:4]
     moved, residual, seen = refs[4:7]
-    taken, pieces, box, message, high, low, field, echo, weight = refs[7:16]
-    sent, heard, base, turn_row, turn_column, order, order_back = refs[16:23]
-    (in_got, in_sent, pair_got, pair_sent, back_got, back_sent, out_got, out_sent) = refs[23:31]
-    (weight_got, weight_sent, seen_got, seen_sent, load, kept, left_sent, left_got) = refs[31:]
+    pieces, box, message, high, low, field, echo, weight = refs[7:15]
+    sent, heard, base, turn_row, turn_column, order, order_back = refs[15:22]
+    (in_got, in_sent, pair_got, pair_sent, back_got, back_sent, out_got, out_sent) = refs[22:30]
+    (weight_got, weight_sent, seen_got, seen_sent, load, kept, left_sent, left_got, again) = refs[30:]
     groups = hearers * layers
     devices = senders * groups
     slab, wide = spectrum.shape[2:]
@@ -356,7 +356,7 @@
 
     for n in range(chunks):
         to_group(
-            lambda g: [(spectrum.at[:, g, chunk(n), :], taken.at[rx, fq, :, chunk(n), :])], in_sent.at[n], in_got.at[n]
+            lambda g: [(spectrum.at[:, g, chunk(n), :], moved.at[:, mine, chunk(n), :])], in_sent.at[n], in_got.at[n]
         )
     for shift in range(senders):
         other = lax.rem(tx + shift, senders)
@@ -436,14 +436,14 @@
                 for h in range(hearers):
                     where = aligned(h * (wide // lanes) + span, lanes)
                     zr, zi = phase_of(sent, heard, g * local + f, down, where)
-                    ar = taken[h, layers - 1, per - 1, down, across]
-                    ai = taken[h, layers - 1, planes - 1, down, across]
+                    ar = moved[per - 1, h * layers + layers - 1, down, across]
+                    ai = moved[planes - 1, h * layers + layers - 1, down, across]
                     for j in range(layers * per - 1, -1, -1):
                         ar, ai = ar * zr + ai * zi, ai * zr - ar * zi
                         if j:
                             q, d = divmod(j - 1, per)
-                            ar = ar + taken[h, q, d, down, across]
-                            ai = ai + taken[h, q, per + d, down, across]
+                            ar = ar + moved[d, h * layers + q, down, across]
+                            ai = ai + moved[per + d, h * layers + q, down, across]
                     parts.append((ar, ai))
                 for s, (real, imag) in enumerate(mix(parts, 1.0)):
                     cr, ci = turn_row[2 * s : 2 * s + 1, across], turn_row[2 * s + 1 : 2 * s + 2, across]
@@ -649,7 +649,7 @@
         )
 
     for n in range(chunks):
-        settle(taken.at[:, :, :, chunk(n), :], in_got.at[n])
+        settle(moved.at[:, :, chunk(n), :], in_got.at[n])
         make_pairs(0, n)
         send_pairs(0, n)
         if n:
@@ -680,6 +680,26 @@
             gradient(f, n)
             if f == local - 1:
                 send_out(n)
+    for n in range(chunks):
+        for p in range(planes):
+            for k in range(senders):
+                near(
+                    spectrum.at[p, :, chunk(n), pl.ds(k * strip, strip)],
+                    pieces.at[pl.ds((p * senders + k) * groups, groups), chunk(n), :],
+                    again.at[n],
+                )
+    for n in range(chunks):
+        settle(pieces.at[:, chunk(n), :], again.at[n])
+        settle(moved.at[:, :, chunk(n), :], out_got.at[n])
+
+        def add(t, carry):
+            p, g = t // groups, t % groups
+            for k in range(senders):
+                across = slice(k * strip, (k + 1) * strip)
+                moved[p, g, chunk(n), across] += pieces[(p * senders + k) * groups + g, chunk(n), :]
+            return carry
+
+        lax.fori_loop(0, planes * groups, add, 0)
     for f in range(local):
         settle_left(f)
     for n in range(chunks):
@@ -687,7 +707,6 @@
         for f in range(local):
             settle(message.at[pl.ds(0, (devices - 1) * 2), chunk(n), :], back_sent.at[f, n])
         settle(box.at[pl.ds(0, (groups - 1) * senders * planes), chunk(n), :], out_sent.at[n])
-        settle(moved.at[:, :, chunk(n), :], out_got.at[n])
     settle(weights.at[:, pl.ds(0, strip * (senders - 1))], weight_sent)
     settle(seen, seen_sent)
     for f in range(local):
@@ -722,14 +741,13 @@
     moved, residual, _ = pl.pallas_call(
         lambda *refs: whole_kernel(sizes, refs),
         in_specs=[anywhere] * 3 + [inside],
-        out_specs=[anywhere] * 3,
+        out_specs=[inside] + [anywhere] * 2,
         out_shape=[
-            jax.ShapeDtypeStruct(blocks.shape, jnp.float32),
+            pltpu.VMEM(blocks.shape, jnp.float32),
             jax.ShapeDtypeStruct(measured.shape, jnp.float32),
             jax.ShapeDtypeStruct((senders - 1, 2, local, rows_sent, strip), jnp.float32),
         ],
         scratch_shapes=[
-            floats(hearers, layers, 2 * per, slab, rows_heard),
             floats(count, slab, strip),
             floats(count, slab, strip),
             floats(count, slab, strip),
@@ -750,10 +768,11 @@
         + [sems((local, chunks))] * 4
         + [sems((chunks,))] * 2
         + [sems] * 4
-        + [sems((local,))] * 4,
+        + [sems((local,))] * 4
+        + [sems((chunks,))],
         compiler_params=pltpu.CompilerParams(vmem_limit_bytes=limit, has_side_effects=True),
     )(blocks, measured, weights, wavenumber.reshape(1, -1))
-    return ((blocks + moved).reshape(spectrum.shape), residual)
+    return (moved.reshape(spectrum.shape), residual)
 
 
 def fits(mesh, sent, heard):

time: 762 us -> 753 us (0.988)
  other arithmetic: 15.9 us -> 3.74 us
    add x1 -> x0, other arithmetic: 12.1 us -> none  [per_device_whole(): return ((blocks + moved).reshape(spectrum.shape), residual)]
where the time goes in v4:
time: 753 us; the launch traced here: 752 us
  Pallas kernels  738 us (98%)
  local copies, waits for them, and re-layouts  9.91 us (1%)
    pallas_call x1, Pallas kernels, per_device_whole(): pl.pallas_call(lambda *refs: whole_kernel(sizes, refs), in_specs=[anywher...  738 us

profile of v4, /device:TPU:19, one launch (start us, length us, event | category | flops | bytes accessed | tf_op | source)
XLA Modules:
  0.0 752.4 jit_solution(8756021307899313563)
XLA Ops:
  0.6 0.7 convert_element_type.3
  1.4 0.8 bitcast_multiply_fusion.1
  2.2 0.1 copy.9
  2.3 2.2 bitcast_multiply_fusion.refs_2_
  4.5 738.1 %shard_map.77 = (f32[4,16,64,512]{3,2,1,0:T(8,128)S(1)}, f32[2,2,1024,512]{3,2,1,0:T(8,128)}, f32[1,2,2,1024,256]{4,3,2,1,0:T(8,128)}) custom-call(f32[4,16,64,512]{3,2,1,0:T(8,128)} %bitcast.8, f32[2,2,1024,512]{3,2,1,0:T(8,128)} %refs_1_.1, f32[1024,512]{1,0:T(8,128)} %bitcast_multiply_fusion.refs_2_, f32[1,8]{1,0:T(1,128)} %bitcast.9), custom_call_target="tpu_custom_call" | custom-call | tf_op jit(solution)/shard_map/pallas_call | solution.py:741
  742.6 0.0 copy-start
  742.6 4.3 copy.12
  746.9 2.1 copy-done
  749.0 3.4 copy.13
Async XLA Ops:
  742.6 6.4 copy-start
